TPU v7x, 32 devices: a whole 2x2x4 slice. The times are simulated.
32 devices in a mesh: child: 2 (over y), row: 4 (over x, core), col: 4 (over z).
Axes of the slice: x: 2, y: 2, z: 4, core: 2. Of those that a mesh axis runs over, the one named last changes fastest.
Arguments:
- child_blocks: float32 [2, 4096, 4096], P('child', 'row', 'col'), as said below
- child_panels: bfloat16 [2, 4096, 1024], P('child', 'row'), may hold values from -0.1875 to 0.1875
- child_patterns: int32 [2, 16, 16], replicated, may hold values from 0 to 1, as said below
- child_maps: int32 [2, 16], replicated, may hold values from 0 to 23, as said below
- parent_place: int32 [24], replicated, may hold values from 0 to 23, as said below
- parent_front: float32 [6144, 6144], P(('child', 'row'), 'col'), as said below
Outputs:
- factored: float32 [6144, 6144], P(('child', 'row'), 'col')
Inputs may be any that keep to these rules, and one draw needn't show every extreme that they name: `parent_place`: a permutation. The entries of one child are distinct; within each aligned block of 4 entries of one child, the values parent_place[child_maps[c, i]] // 6 are distinct. `child_patterns`: symmetric in its two tile dimensions, with ones on the diagonal. `child_blocks`: each child's block is symmetric. `parent_front`: symmetric; the diagonal entries inside stored tiles (parent_place[0], parent_place[0]) and (parent_place[1], parent_place[1]) lie between 200 and 400.
All inputs are finite; a program needn't handle non-finite values.
Results may differ from a plain program's by a relative error of at most 0.0003.
Values may be sent and summed in bfloat16 or wider, within the bound.
A program may use at most 128 MiB of HBM per device.

v0:
```python
import jax
import jax.numpy as jnp
from jax import lax
from jax.sharding import PartitionSpec as P

TILE = 256
PANEL = 512


def spread(block, axis, source):
    block = jnp.where(lax.axis_index(axis) == source, block, jnp.zeros_like(block))
    return lax.psum(block, axis)


def lookup(lookup_table, positions):
    matches = positions[:, None] == jnp.arange(lookup_table.shape[0], dtype=jnp.int32)[None, :]
    return jnp.sum(jnp.where(matches, lookup_table[None, :], 0), axis=1)


def find_owner(slot_list, targets):
    matches = targets[:, None] == slot_list[None, :]
    located = jnp.any(matches, axis=1)
    chosen = jnp.sum(
        jnp.where(matches, jnp.arange(slot_list.shape[0], dtype=jnp.int32)[None, :], 0), axis=1
    )
    return (located, chosen)


def select_tiles(source, located, chosen, axis_pos):
    selected = jnp.take(source, chosen, axis=axis_pos)
    dims_shape = [1] * source.ndim
    dims_shape[axis_pos] = located.shape[0]
    return jnp.where(located.reshape(dims_shape), selected, jnp.zeros((), source.dtype))


def body(child_blocks, child_panels, child_patterns, child_maps, parent_place, parent_front):
    child_index = lax.axis_index("child")
    row_index = lax.axis_index("row")
    col_index = lax.axis_index("col")
    row_count = lax.axis_size("row")
    col_count = lax.axis_size("col")
    group_count = lax.axis_size(("child", "row"))
    own_block = child_blocks[0]
    block_width = own_block.shape[0]
    tiles_dev = block_width // TILE
    rows_dev = parent_front.shape[0] // TILE
    cols_dev = parent_front.shape[1] // TILE
    own_panel = child_panels[0]
    partner = spread(own_panel, "row", col_index)
    product = lax.dot_general(
        own_panel, partner, (((1,), (1,)), ((), ())), preferred_element_type=jnp.float32
    )
    pattern = lax.dynamic_index_in_dim(child_patterns, child_index, 0, keepdims=False)
    pattern = lax.dynamic_slice(
        pattern, (row_index * tiles_dev, col_index * tiles_dev), (tiles_dev, tiles_dev)
    ).astype(jnp.float32)
    update = (own_block - product).reshape(tiles_dev, TILE, tiles_dev, TILE) * pattern[
        :, None, :, None
    ]
    slot_table = jnp.stack(
        [lookup(parent_place, child_maps[0]), lookup(parent_place, child_maps[1])]
    )
    own_slots = lax.dynamic_index_in_dim(slot_table, child_index, 0, keepdims=False)
    row_slots = lax.dynamic_slice_in_dim(own_slots, row_index * tiles_dev, tiles_dev)
    col_slots = lax.dynamic_slice_in_dim(own_slots, col_index * tiles_dev, tiles_dev)
    group_index = child_index * row_count + row_index
    row_targets = group_index * rows_dev + jnp.arange(rows_dev, dtype=jnp.int32)
    col_targets = col_index * cols_dev + jnp.arange(cols_dev, dtype=jnp.int32)
    group_ids = jnp.arange(group_count, dtype=jnp.int32)
    column_ids = jnp.arange(col_count, dtype=jnp.int32)
    located, chosen = find_owner(col_slots // cols_dev, column_ids)
    outgoing = select_tiles(update.reshape(block_width, tiles_dev, TILE), located, chosen, 1)
    incoming = lax.all_to_all(outgoing, "col", split_axis=1, concat_axis=1, tiled=True)
    located, chosen = find_owner(own_slots, col_targets)
    placed = select_tiles(incoming, located, chosen // tiles_dev, 1).reshape(
        tiles_dev, TILE, cols_dev * TILE
    )
    located, chosen = find_owner(row_slots // rows_dev, group_ids)
    outgoing_rows = select_tiles(placed, located, chosen, 0)
    incoming_rows = lax.all_to_all(
        outgoing_rows, ("child", "row"), split_axis=0, concat_axis=0, tiled=True
    )
    contribution = jnp.zeros((rows_dev, TILE, cols_dev * TILE), jnp.float32)
    for member in range(2):
        located, chosen = find_owner(slot_table[member], row_targets)
        sender = member * row_count + chosen // tiles_dev
        contribution = contribution + select_tiles(incoming_rows, located, sender, 0)
    assembled = parent_front + contribution.reshape(parent_front.shape)
    panel_slots = parent_place[0:2]
    col_local = panel_slots // cols_dev == col_index
    col_pos = panel_slots % cols_dev
    row_local = panel_slots // rows_dev == group_index
    row_pos = panel_slots % rows_dev
    front_tiles = assembled.reshape(rows_dev * TILE, cols_dev, TILE)
    column = select_tiles(front_tiles, col_local, col_pos, 1).reshape(rows_dev * TILE, PANEL)
    diagonal_part = select_tiles(
        column.reshape(rows_dev, TILE, PANEL), row_local, row_pos, 0
    ).reshape(PANEL, PANEL)
    panel_column = lax.psum(column, "col")
    diagonal_block = lax.psum(diagonal_part, ("child", "row", "col"))
    factor = jnp.linalg.cholesky(diagonal_block)
    panel_rows = lax.linalg.triangular_solve(
        factor, panel_column, left_side=False, lower=True, transpose_a=True
    )
    halves = []
    for member in range(2):
        halves.append(spread(panel_rows, ("child", "row"), 2 * col_index + member))
    panel_cols = jnp.concatenate(halves, axis=0)
    result = assembled - lax.dot_general(
        panel_rows,
        panel_cols,
        (((1,), (1,)), ((), ())),
        precision=lax.Precision.HIGHEST,
        preferred_element_type=jnp.float32,
    )
    result_tiles = result.reshape(rows_dev * TILE, cols_dev, TILE)
    tile_positions = jnp.arange(cols_dev, dtype=jnp.int32)
    for member in range(2):
        chosen_cols = jnp.logical_and(tile_positions == col_pos[member], col_local[member])
        result_tiles = jnp.where(
            chosen_cols[None, :, None],
            panel_rows[:, None, member * TILE : (member + 1) * TILE],
            result_tiles,
        )
    return result_tiles.reshape(parent_front.shape)


def solution(mesh):
    return jax.shard_map(
        body,
        mesh=mesh,
        in_specs=(
            P("child", "row", "col"),
            P("child", "row", None),
            P(),
            P(),
            P(),
            P(("child", "row"), "col"),
        ),
        out_specs=P(("child", "row"), "col"),
        check_vma=False,
    )
```

profile of v0, /device:TPU:0, one launch (start us, length us, event | category | flops | bytes accessed | tf_op | source)
XLA Modules:
  0.0 784.9 jit_solution(8666867808019406183)
XLA Ops:
  6.5 3.0 bitcast_select_fusion
  10.8 5.5 copy.61
  16.7 47.2 %all-reduce.7.cloned.1.call-done = bf16[1024,1024]{1,0:T(8,128)(2,1)} async-done(((bf16[1024,1024]{1,0:T(8,128)(2,1)}), bf16[1024,1024]{1,0:T(8,128)(2,1)}) %all-reduce.7.cloned.1.call-update) | async-done | bytes 2097168 | tf_op jit(solution)/shard_map/psum | solution.py:12
  63.9 5.2 bitcast_subtract_fusion
  69.1 2.5 broadcast_multiply_fusion
  71.6 4.9 gather_fusion
  76.5 5.2 select_bitcast_fusion
  81.7 4.9 all-to-all-start
  87.4 92.4 %all-to-all-done = f32[1024,4,256]{0,2,1:T(8,128)} async-done(((f32[1024,4,256]{0,2,1:T(8,128)}), f32[1024,4,256]{0,2,1:T(8,128)}, u32[]{:S(2)}, u32[]{:S(2)}) %all-to-all-start) | async-done | bytes 4194336 | tf_op jit(solution)/shard_map/all_to_all | solution.py:73
  179.8 5.8 gather_fusion.1
  185.6 8.1 %gather.35 = f32[4,256,1536]{1,0,2:T(4,128)} reshape(f32[1024,6,256]{0,2,1:T(8,128)} %bitcast.115) | data formatting | bytes 12582912 | tf_op jit(solution)/shard_map/jit(_take)/gather | solution.py:30
  193.7 7.6 copy.63
  201.3 6.3 select_select_fusion.1
  207.6 8.6 %gather_fusion.2 = f32[8,256,1536]{2,1,0:T(8,128)} fusion(f32[4,256,1536]{2,1,0:T(8,128)} %select_select_fusion.1, s32[1024]{0:T(1024)S(1)} %pad_clamp_fusion.4), kind=kCustom, calls=%fused_computation.4 | custom fusion | bytes 25165856 | tf_op jit(solution)/shard_map/jit(_take)/gather | solution.py:30
  216.2 11.4 %select_select_fusion = f32[8,256,1536]{2,1,0:T(8,128)} fusion(f32[8,256,1536]{2,1,0:T(8,128)} %gather_fusion.2, pred[8]{0:T(512)(128)(4,1)S(1)} %compare_and_fusion.6, pred[8]{0:T(512)(128)(4,1)S(1)} %fusion.35), kind=kLoop, calls=%fused_computation.9 | loop fusion | flops 6291456 | bytes 25165840 | tf_op jit(solution)/shard_map/jit(_where)/select_n | solution.py:33
  227.6 5.3 all-to-all-start.1
  234.4 137.6 %all-to-all-done.1 = f32[8,256,1536]{2,1,0:T(8,128)} async-done(((f32[8,256,1536]{2,1,0:T(8,128)}), f32[8,256,1536]{2,1,0:T(8,128)}, u32[]{:S(2)}, u32[]{:S(2)}) %all-to-all-start.1) | async-done | bytes 12582944 | tf_op jit(solution)/shard_map/all_to_all | solution.py:80
  372.0 7.5 gather_fusion.5
  379.5 7.7 gather_fusion.6
  387.2 5.1 fusion
  392.3 3.2 bitcast_add_fusion
  395.5 6.0 copy.64
  401.6 6.1 copy.65
  407.7 3.0 gather_fusion.3
  410.7 2.4 copy.67
  413.1 2.5 gather.39
  417.0 2.0 gather_fusion.4
  420.3 2.3 select_select_fusion.7
  424.9 125.9 %all-reduce.11.cloned.1.call-done = f32[512,512]{0,1:T(8,128)} async-done(((f32[512,512]{0,1:T(8,128)}), f32[512,512]{0,1:T(8,128)}) %all-reduce.11.cloned.1.call-update) | async-done | bytes 1048592 | tf_op jit(solution)/shard_map/psum | solution.py:100
  550.8 1.6 copy.69
  553.8 11.7 %cholesky.102 = f32[128,128]{1,0:T(8,128)S(1)} custom-call(f32[128,128]{1,0:T(8,128)S(1)} %cholesky.260), custom_call_target="Cholesky" | custom-call | tf_op jit(solution)/shard_map/jit(cholesky)/cholesky | solution.py:101
  565.5 9.8 %custom-call.30 = f32[1,128,128]{1,2,0:T(8,128)S(1)} custom-call(f32[1,128,128]{2,1,0:T(8,128)S(1)} %get-tuple-element.63), custom_call_target="InvertDiagBlocksLowerTriangular" | custom-call | tf_op jit(solution)/shard_map/jit(cholesky)/cholesky | solution.py:101
  576.0 11.7 %cholesky.213 = f32[128,128]{1,0:T(8,128)S(1)} custom-call(f32[128,128]{1,0:T(8,128)S(1)} %cholesky.264), custom_call_target="Cholesky" | custom-call | tf_op jit(solution)/shard_map/jit(cholesky)/cholesky | solution.py:101
  588.1 10.0 %custom-call.31 = f32[1,128,128]{1,2,0:T(8,128)S(1)} custom-call(f32[1,128,128]{2,1,0:T(8,128)S(1)} %get-tuple-element.61), custom_call_target="InvertDiagBlocksLowerTriangular" | custom-call | tf_op jit(solution)/shard_map/jit(cholesky)/cholesky | solution.py:101
  599.2 11.7 %cholesky.234 = f32[128,128]{1,0:T(8,128)S(1)} custom-call(f32[128,128]{1,0:T(8,128)S(1)} %cholesky.269), custom_call_target="Cholesky" | custom-call | tf_op jit(solution)/shard_map/jit(cholesky)/cholesky | solution.py:101
  611.1 9.8 %custom-call.32 = f32[1,128,128]{1,2,0:T(8,128)S(1)} custom-call(f32[1,128,128]{2,1,0:T(8,128)S(1)} %get-tuple-element.59), custom_call_target="InvertDiagBlocksLowerTriangular" | custom-call | tf_op jit(solution)/shard_map/jit(cholesky)/cholesky | solution.py:101
  621.7 11.9 %cholesky.251 = f32[128,128]{1,0:T(8,128)S(1)} custom-call(f32[128,128]{1,0:T(8,128)S(1)} %convolution_subtract_fusion.5), custom_call_target="Cholesky" | custom-call | tf_op jit(solution)/shard_map/jit(cholesky)/cholesky | solution.py:101
  638.9 8.0 %while.1 = (s32[]{:T(128)}, f32[512,512]{0,1:T(8,128)S(1)}, s32[4,2]{0,1:T(2,128)S(1)}, f32[4,128,128]{2,1,0:T(8,128)S(1)}, s32[]{:T(128)}) while((s32[]{:T(128)}, f32[512,512]{0,1:T(8,128)S(1)}, s32[4,2]{0,1:T(2,128)S(1)}, f32[4,128,128]{2,1,0:T(8,128)S(1)}, s32[]{:T(128)}) %tuple.46), condition=%wide.while_cond, body=%wide.while_body.sunk | while | flops 2 | bytes 393321 | solution.py:102
  646.9 39.3 %custom-call.33 = f32[4,128,128]{1,2,0:T(8,128)S(1)} custom-call(f32[4,128,128]{2,1,0:T(8,128)S(1)} %get-tuple-element.13), custom_call_target="InvertDiagBlocksLowerTriangular" | custom-call | tf_op jit(solution)/shard_map/triangular_solve | solution.py:102
  689.8 1.6 convolution_subtract_fusion.2
  692.0 1.9 convolution_subtract_fusion
  694.5 1.8 broadcast_select_fusion.1
  700.4 2.6 broadcast_in_dim.369
  702.9 6.1 copy.81
  709.0 2.6 broadcast_in_dim.364
  711.7 6.2 copy.82
  717.9 46.9 %all-reduce.13.cloned.1.call-done = (f32[768,512]{0,1:T(8,128)}, f32[768,512]{0,1:T(8,128)}) async-done(((f32[768,512]{0,1:T(8,128)}, f32[768,512]{0,1:T(8,128)}), (f32[768,512]{0,1:T(8,128)}, f32[768,512]{0,1:T(8,128)})) %all-reduce.13.cloned.1.call-update) | async-done | bytes 3145744 | tf_op jit(solution)/shard_map/psum | solution.py:12
  764.8 13.1 %select_select_fusion.4 = f32[768,1536]{1,0:T(8,128)} fusion(f32[768,1536]{1,0:T(8,128)} %copy.82, f32[768,1536]{1,0:T(8,128)} %copy.81, f32[768,1536]{1,0:T(8,128)} %bitcast_add_fusion, f32[768,512]{0,1:T(8,128)} %get-tuple-element.44, f32[768,512]{0,1:T(8,128)} %get-tuple-element.45, pred[1536]{0:T(1024)(128)(4,1)S(1)} %broadcast_in_dim.367, ...), kind=kOutput, calls=%fused_computation.15 | convolution fusion | flops 7253262336 | bytes 23596032 | tf_op jit(solution)/shard_map/dot_general | solution.py:109
  (138 shorter events, 32.3 us)
Async XLA Ops:
  6.5 3.1 copy-start.2
  6.5 4.1 copy-start.1
  6.5 57.3 %all-reduce.7.cloned.1.call-start = ((), (), s32[]{:S(2)}) async-start(), calls=%async_computation.2 | async-start | bytes 4194304 | tf_op jit(solution)/shard_map/psum | solution.py:12
  10.8 53.1 %copy-start = (bf16[1,1024,1024]{2,1,0:T(8,128)(2,1)S(1)}, bf16[1,1024,1024]{2,1,0:T(8,128)(2,1)}, u32[]{:S(2)}) copy-start(bf16[1,1024,1024]{2,1,0:T(8,128)(2,1)} %param.9) | copy-start | bytes 6291460
  81.7 98.1 %all-to-all-start = ((f32[1024,4,256]{0,2,1:T(8,128)}), f32[1024,4,256]{0,2,1:T(8,128)}, u32[]{:S(2)}, u32[]{:S(2)}) async-start(f32[1024,4,256]{0,2,1:T(8,128)} %select_bitcast_fusion), calls=%async_computation | async-start | bytes 8388608 | tf_op jit(solution)/shard_map/all_to_all | solution.py:73
  227.6 144.3 %all-to-all-start.1 = ((f32[8,256,1536]{2,1,0:T(8,128)}), f32[8,256,1536]{2,1,0:T(8,128)}, u32[]{:S(2)}, u32[]{:S(2)}) async-start(f32[8,256,1536]{2,1,0:T(8,128)} %select_select_fusion), calls=%async_computation.1 | async-start | bytes 25165824 | tf_op jit(solution)/shard_map/all_to_all | solution.py:80
  233.0 317.8 %all-reduce.11.cloned.1.call-start = ((), (), s32[]{:S(2)}) async-start(), calls=%async_computation.4 | async-start | bytes 2097152 | tf_op jit(solution)/shard_map/psum | solution.py:100
  379.5 12.8 %slice-start = ((s8[4718592]{0:T(1024)(128)(4,1)}), s8[524288]{0:T(1024)(128)(4,1)S(1)}, s32[]{:S(2)}) async-start(s8[4718592]{0:T(1024)(128)(4,1)} %bitcast.121), calls=%async_computation.6 | async-start | bytes 1048576
  387.2 5.1 slice-start.1
  422.7 263.6 %all-reduce.9.cloned.1.call-start = ((), (), s32[]{:S(2)}) async-start(), calls=%async_computation.3 | async-start | bytes 3145728 | tf_op jit(solution)/shard_map/psum | solution.py:99
  424.7 340.1 %all-reduce.13.cloned.1.call-start = ((), (), s32[]{:S(2)}) async-start(), calls=%async_computation.5 | async-start | bytes 6291456 | tf_op jit(solution)/shard_map/psum | solution.py:12
Sparse Core Ops, SparseCore 0:
  9.7 54.0 all-reduce.6
  422.8 127.9 all-reduce.10
  553.1 67.9 all-reduce.8
  696.5 68.2 all-reduce.12
where the time goes:
time: 793 us; the launch traced here: 785 us
  waiting for transfers between devices  450 us (57%)
  other arithmetic  169 us (21%)
  local copies, waits for them, and re-layouts  109 us (14%)
  matrix products  28.8 us (4%)
  between operations  16.6 us (2%)
  starting transfers between devices  11 us (1%)
    all_to_all x1, waiting for transfers between devices, body(): lax.all_to_all(outgoing_rows, ('child', 'row'), split_axis=0, concat_axis...  138 us
    psum x1, waiting for transfers between devices, body(): diagonal_block = lax.psum(diagonal_part, ('child', 'row', 'col'))  126 us
    psum x2, waiting for transfers between devices, spread(): return lax.psum(block, axis)  94.1 us
    all_to_all x1, waiting for transfers between devices, body(): lax.all_to_all(outgoing, 'col', split_axis=1, concat_axis=1, tiled=True)  92.4 us
    another operation x15, other arithmetic, body(): factor = jnp.linalg.cholesky(diagonal_block)  79.4 us
    gather x13, local copies, waits for them, and re-layouts, select_tiles(): selected = jnp.take(source, chosen, axis=axis_pos)  61.9 us
    another operation x5, other arithmetic, body(): lax.linalg.triangular_solve(factor, panel_column, left_side=False, lower=...  39.6 us
    select_n x6, other arithmetic, select_tiles(): jnp.where(located.reshape(dims_shape), selected, jnp.zeros((), source.dty...  28 us
  transfers between devices with their start and end apart: 6, of which 5 were waited for; matrix products, arithmetic and copies ran while one was open for 21% of the time, Pallas kernels for 0%

commit v1 on v0

v1 whole, which is shorter than its diff:
```python
import functools

import jax
import jax.numpy as jnp
from jax import lax
from jax.experimental import pallas as pl
from jax.experimental.pallas import tpu as pltpu
from jax.sharding import Mesh, PartitionSpec as P

TILE = 256
F32 = jnp.float32
BF16 = jnp.bfloat16
NT = (((1,), (1,)), ((), ()))
TN = (((0,), (0,)), ((), ()))


def dot(a, b, dims):
    return lax.dot_general(a, b, dims, preferred_element_type=F32)


def split(x):
    hi = x.astype(BF16)
    return hi, (x - hi.astype(F32)).astype(BF16)


def dot3(a, b, dims):
    ah, al = split(a)
    bh, bl = split(b)
    return dot(ah, bh, dims) + (dot(ah, bl, dims) + dot(al, bh, dims))


def tile_call(kernel, grid, tables, operands, in_specs, out_shape, out_spec, name, cost=None, scratch=()):
    return pl.pallas_call(
        kernel,
        grid_spec=pltpu.PrefetchScalarGridSpec(
            num_scalar_prefetch=len(tables), grid=grid, in_specs=in_specs, out_specs=out_spec,
            scratch_shapes=list(scratch),
        ),
        out_shape=out_shape,
        name=name,
        cost_estimate=cost,
    )(*tables, *operands)


def pick_kernel(idx, loc, src, out):
    ok = loc[pl.program_id(0)] != 0
    out[0] = jnp.where(ok, src[...], jnp.zeros_like(src))


def diag_kernel(t, blk, front, ea, eb, out):
    k = pl.program_id(0) * 2 + pl.program_id(1)
    x = jnp.where(t[4, k] != 0, blk[...], 0.0) + jnp.where(t[5, k] != 0, front[...], 0.0)
    out[...] = x - jnp.where(t[6, k] != 0, dot(ea[...], eb[...], NT), 0.0)


def update_kernel(rows, fac, raw, panel, partner, out):
    f = fac[pl.program_id(0), pl.program_id(1)]
    u = raw[0] - dot(panel[...], partner[0], NT)
    out[0] = jnp.where(f != 0, u, 0.0)


def strip_kernel(t, upd, front, out):
    a, q = pl.program_id(0), pl.program_id(1)
    k = a * pl.num_programs(1) + q
    out[...] = jnp.where(t[2, k] != 0, upd[0], 0.0) + jnp.where(t[4, k] != 0, front[...], 0.0)


def final_kernel(t, front, a0, b0, a1, b1, wr, wc, out):
    k = pl.program_id(0) * pl.num_programs(1) + pl.program_id(1)
    panel = t[12, k]

    @pl.when(panel == 0)
    def _():
        x = front[...]
        for m, src in enumerate((a0, b0, a1, b1)):
            x = x + jnp.where(t[8 + m, k] != 0, src[0], 0.0)
        out[...] = x - dot3(wr[...], wc[...], TN)

    @pl.when(panel == 1)
    def _():
        out[...] = wr[:TILE, :].T

    @pl.when(panel == 2)
    def _():
        out[...] = wr[TILE:, :].T


def body(child_blocks, child_panels, child_patterns, child_maps, parent_place, parent_front):
    ci = lax.axis_index("child")
    rx = lax.axis_index("rx")
    core = lax.axis_index("core")
    col = lax.axis_index("col")
    cores = lax.axis_size("core")
    rxn = lax.axis_size("rx")
    row = rx * cores + core
    rown = rxn * cores
    chips = lax.axis_size("child") * rxn
    chip = ci * rxn + rx
    group = ci * rown + row
    block = child_blocks[0]
    own = child_panels[0]
    depth = own.shape[1]
    width = block.shape[0]
    td = width // TILE
    blocks = child_maps.shape[1] // td
    rd = parent_front.shape[0] // TILE
    cd = parent_front.shape[1] // TILE
    slots_n = parent_place.shape[0]
    i32 = jnp.int32

    slots = jnp.sum(
        jnp.where(child_maps[:, :, None] == jnp.arange(slots_n, dtype=i32), parent_place, 0), axis=2
    )
    tiles = jnp.arange(child_maps.shape[1], dtype=i32)
    hit = slots[:, None, :] == jnp.arange(slots_n, dtype=i32)[None, :, None]
    inv = jnp.sum(jnp.where(hit, tiles + 1, 0), axis=2) - 1
    mine = lax.dynamic_index_in_dim(slots, ci, 0, keepdims=False).reshape(blocks, td)
    inv_own = lax.dynamic_index_in_dim(inv, ci, 0, keepdims=False)
    pat = lax.dynamic_index_in_dim(child_patterns, ci, 0, keepdims=False)
    m = (mine // cd)[:, None, :] == jnp.arange(chips, dtype=i32)[None, :, None]
    which = jnp.sum(jnp.where(m, jnp.arange(td, dtype=i32), 0), axis=2)
    there = jnp.any(m, axis=2).astype(i32)
    row_tile = lax.dynamic_index_in_dim(which, row, 0, keepdims=False)
    row_ok = lax.dynamic_index_in_dim(there, row, 0, keepdims=False)
    out_tile = lax.dynamic_index_in_dim(which, col, 0, keepdims=False)
    out_ok = lax.dynamic_index_in_dim(there, col, 0, keepdims=False)
    in_tile = lax.dynamic_index_in_dim(which, col, 1, keepdims=False)
    in_ok = lax.dynamic_index_in_dim(there, col, 1, keepdims=False)
    e = parent_place[:2]
    ie = inv_own[e]

    outgoing = tile_call(
        pick_kernel, (blocks,), (out_tile, out_ok), (block,),
        [pl.BlockSpec((width, TILE), lambda z, i, l: (0, i[z]))],
        jax.ShapeDtypeStruct((blocks, width, TILE), F32),
        pl.BlockSpec((1, width, TILE), lambda z, i, l: (z, 0, 0)), "pick",
    )
    raw = lax.all_to_all(outgoing, "col", split_axis=0, concat_axis=0, tiled=True)

    part = lax.dynamic_slice(own, (row_tile[col] * TILE, 0), (TILE, depth))
    part = jnp.where(row_ok[col] != 0, part, jnp.zeros_like(part))

    e_here = jnp.logical_and(ie >= 0, ie // td == row)
    e_rows = jnp.concatenate([
        jnp.where(e_here[a], lax.dynamic_slice(own, ((ie[a] % td) * TILE, 0), (TILE, depth)), jnp.zeros((), BF16))
        for a in range(2)
    ])
    e_all = lax.psum(e_rows, ("rx", "core"))
    partner = lax.all_gather(part, ("rx", "core"), axis=0)
    pair_a = jnp.array([0, 0, 1, 1], i32)
    pair_b = jnp.array([0, 1, 0, 1], i32)
    ia, ib, ea, eb = ie[pair_a], ie[pair_b], e[pair_a], e[pair_b]
    live = (ia >= 0) & (ib >= 0) & (pat[jnp.maximum(ia, 0), jnp.maximum(ib, 0)] != 0)
    table = jnp.stack([
        jnp.maximum(ia, 0) % td, jnp.maximum(ib, 0) % td, ea % rd, eb % cd,
        live & (ia // td == row) & (ib // td == col),
        (ea // rd == group) & (eb // cd == col),
        live & (row == 0) & (col == 0),
    ]).astype(i32)
    diag_part = tile_call(
        diag_kernel, (2, 2), (table,), (block, parent_front, e_all, e_all),
        [
            pl.BlockSpec((TILE, TILE), lambda a, b, t: (t[0, a * 2 + b], t[1, a * 2 + b])),
            pl.BlockSpec((TILE, TILE), lambda a, b, t: (t[2, a * 2 + b], t[3, a * 2 + b])),
            pl.BlockSpec((TILE, depth), lambda a, b, t: (a, 0)),
            pl.BlockSpec((TILE, depth), lambda a, b, t: (b, 0)),
        ],
        jax.ShapeDtypeStruct((2 * TILE, 2 * TILE), F32),
        pl.BlockSpec((TILE, TILE), lambda a, b, t: (a, b)), "diag",
    )
    diagonal = lax.psum(diag_part, ("child", "rx", "core", "col"))
    factor = jnp.linalg.cholesky(diagonal)
    inverse = lax.linalg.triangular_solve(
        factor, jnp.eye(2 * TILE, dtype=F32), left_side=True, lower=True
    )

    col_ids = jnp.arange(blocks, dtype=i32) * td + in_tile
    factors = pat[row * td + row_tile][:, col_ids] * row_ok[:, None] * in_ok[None, :]
    update = tile_call(
        update_kernel, (chips, blocks), (row_tile, factors), (raw, own, partner),
        [
            pl.BlockSpec((1, TILE, TILE), lambda p, b, r, f: (b, r[p], 0)),
            pl.BlockSpec((TILE, depth), lambda p, b, r, f: (r[p], 0)),
            pl.BlockSpec((1, TILE, depth), lambda p, b, r, f: (b, 0, 0)),
        ],
        jax.ShapeDtypeStruct((chips, TILE, blocks * TILE), F32),
        pl.BlockSpec((1, TILE, TILE), lambda p, b, r, f: (p, 0, b)), "update",
    )
    first = lax.all_to_all(update, ("child", "rx"), split_axis=0, concat_axis=0, tiled=True)
    second = lax.ppermute(first, "core", [(k, (k + 1) % 2) for k in range(2)])

    my_cols = lax.dynamic_slice_in_dim(inv, col * cd, cd, 1)
    my_rows = lax.dynamic_slice_in_dim(inv, group * rd, rd, 1)
    cols_own = lax.dynamic_index_in_dim(my_cols, ci, 0, keepdims=False)
    grid_q = jnp.broadcast_to(jnp.arange(cd, dtype=i32), (2, cd))
    e2 = jnp.broadcast_to(e[:, None], (2, cd))
    cols2 = jnp.broadcast_to(cols_own[None, :], (2, cd))
    table = jnp.stack([
        e2 // cd, jnp.maximum(cols2, 0) // td,
        (e_here[:, None] & (cols2 >= 0)),
        e2 % rd, (e2 // rd == group),
    ]).astype(i32).reshape(5, 2 * cd)
    strip_part = tile_call(
        strip_kernel, (2, cd), (table,), (update, parent_front),
        [
            pl.BlockSpec((1, TILE, TILE), lambda a, q, t: (t[0, a * cd + q], 0, t[1, a * cd + q])),
            pl.BlockSpec((TILE, TILE), lambda a, q, t: (t[3, a * cd + q], q)),
        ],
        jax.ShapeDtypeStruct((2 * TILE, cd * TILE), F32),
        pl.BlockSpec((TILE, TILE), lambda a, q, t: (a, q)), "strip",
    )
    strip = lax.psum(strip_part, ("child", "rx", "core"))
    half = lax.dynamic_slice(strip, (0, core * rd * TILE), (2 * TILE, rd * TILE))
    half = lax.psum(jnp.where(chip == col, half, jnp.zeros_like(half)), "col")
    wc = lax.dot_general(inverse, strip, (((1,), (0,)), ((), ())), precision=lax.Precision.HIGHEST)
    wr = lax.dot_general(inverse, half, (((1,), (0,)), ((), ())), precision=lax.Precision.HIGHEST)

    rr = jnp.broadcast_to(my_rows[:, :, None], (2, rd, cd))
    cc = jnp.broadcast_to(my_cols[:, None, :], (2, rd, cd))
    ok = (rr >= 0) & (cc >= 0)
    send_row = jnp.maximum(rr, 0) // td
    same = send_row % cores == core
    send = jnp.arange(2, dtype=i32)[:, None, None] * rxn + send_row // cores
    from_b = jnp.maximum(cc, 0) // td
    lists = []
    for c in range(2):
        for kind in (same, ~same):
            flag = ok[c] & kind[c]
            lists.append((jnp.where(flag, send[c], 0), jnp.where(flag, from_b[c], 0), flag.astype(i32)))
    here = col * cd + jnp.arange(cd, dtype=i32)
    panel = jnp.where(here == e[0], 1, jnp.where(here == e[1], 2, 0))
    rows = [x[n] for n in (0, 1) for x in lists] + [x[2] for x in lists]
    rows.append(jnp.broadcast_to(panel, (rd, cd)))
    table = jnp.stack(rows).reshape(13, rd * cd)

    def from_list(n):
        return pl.BlockSpec(
            (1, TILE, TILE), lambda i, j, t: (t[n, i * cd + j], 0, t[4 + n, i * cd + j])
        )

    return tile_call(
        final_kernel, (rd, cd), (table,), (parent_front, first, second, first, second, wr, wc),
        [pl.BlockSpec((TILE, TILE), lambda i, j, t: (i, j))] + [from_list(n) for n in range(4)] + [
            pl.BlockSpec((2 * TILE, TILE), lambda i, j, t: (0, i)),
            pl.BlockSpec((2 * TILE, TILE), lambda i, j, t: (0, j)),
        ],
        jax.ShapeDtypeStruct(parent_front.shape, F32),
        pl.BlockSpec((TILE, TILE), lambda i, j, t: (i, j)), "final",
    )


def solution(mesh):
    child, row, col = mesh.devices.shape
    cores = child * row // col
    fine = Mesh(mesh.devices.reshape(child, row // cores, cores, col), ("child", "rx", "core", "col"))
    return jax.shard_map(
        body,
        mesh=fine,
        in_specs=(
            P("child", ("rx", "core"), "col"),
            P("child", ("rx", "core"), None),
            P(),
            P(),
            P(),
            P(("child", "rx", "core"), "col"),
        ),
        out_specs=P(("child", "rx", "core"), "col"),
        check_vma=False,
    )
```

time: 793 us -> 531 us (0.67)
  waiting for transfers between devices: 450 us -> 249 us
  local copies, waits for them, and re-layouts: 109 us -> 28.6 us
  Pallas kernels: 0 us -> 55.7 us
  other arithmetic: 169 us -> 136 us
    all_to_all x2, waiting for transfers between devices: 230 us -> 47.8 us  [the longest x1 47.8 us: body(): lax.all_to_all(outgoing, 'col', split_axis=0, concat_axis=0, tiled=True)]
    gather x13 -> x10, local copies, waits for them, and re-layouts: 61.9 us -> 5.13 us  [the longest x4 2.56 us: body(): ia, ib, ea, eb = (ie[pair_a], ie[pair_b], e[pair_a], e[pair_b])]
    pallas_call x0 -> x5, Pallas kernels: none -> 55.7 us  [tile_call(): pl.pallas_call(kernel, grid_spec=pltpu.PrefetchScalarGridSpec(num_scalar_...]
    psum x4, waiting for transfers between devices: 220 us -> 185 us  [the longest x1 96.7 us: body(): diagonal = lax.psum(diag_part, ('child', 'rx', 'core', 'col'))]
    select_n x12 -> x13, other arithmetic: 32.9 us -> 7.98 us  [the longest x1 3.68 us: body(): jnp.where(e_here[a], lax.dynamic_slice(own, (ie[a] % td * TILE, 0), (TILE...]
    broadcast_in_dim x20 -> x2, local copies, waits for them, and re-layouts: 18.2 us -> 0.09 us  [body(): cols2 = jnp.broadcast_to(cols_own[None, :], (2, cd))]
    all_gather x0 -> x1, waiting for transfers between devices: none -> 15.3 us  [body(): partner = lax.all_gather(part, ('rx', 'core'), axis=0)]
    add x4 -> x2, other arithmetic: 8.36 us -> 0.08 us  [the longest x1 0.08 us: body(): send = jnp.arange(2, dtype=i32)[:, None, None] * rxn + send_row // cores]
  transfers between devices with their start and end apart: 6 -> 8, of which waited for: 5 -> 6; matrix products, arithmetic and copies ran while one was open for 21% -> 34% of each run, Pallas kernels for 0% -> 7%
where the time goes in v1:
time: 531 us; the launch traced here: 526 us
  waiting for transfers between devices  249 us (47%)
  other arithmetic  136 us (26%)
  Pallas kernels  55.7 us (10%)
  local copies, waits for them, and re-layouts  28.6 us (5%)
  matrix products  24 us (5%)
  between operations  21.2 us (4%)
  starting transfers between devices  11.7 us (2%)
    psum x1, waiting for transfers between devices, body(): diagonal = lax.psum(diag_part, ('child', 'rx', 'core', 'col'))  96.7 us
    another operation x15, other arithmetic, body(): factor = jnp.linalg.cholesky(diagonal)  79.6 us
    pallas_call x5, Pallas kernels, tile_call(): pl.pallas_call(kernel, grid_spec=pltpu.PrefetchScalarGridSpec(num_scalar_...  55.7 us
    psum x1, waiting for transfers between devices, body(): half = lax.psum(jnp.where(chip == col, half, jnp.zeros_like(half)), 'col')  53.9 us
    all_to_all x1, waiting for transfers between devices, body(): lax.all_to_all(outgoing, 'col', split_axis=0, concat_axis=0, tiled=True)  47.8 us
    another operation x3, other arithmetic, body(): lax.linalg.triangular_solve(factor, jnp.eye(2 * TILE, dtype=F32), left_si...  40.3 us
    psum x1, waiting for transfers between devices, body(): e_all = lax.psum(e_rows, ('rx', 'core'))  18 us
    psum x1, waiting for transfers between devices, body(): strip = lax.psum(strip_part, ('child', 'rx', 'core'))  16.2 us
  transfers between devices with their start and end apart: 8, of which 6 were waited for; matrix products, arithmetic and copies ran while one was open for 34% of the time, Pallas kernels for 7%

profile of v1, /device:TPU:0, one launch (start us, length us, event | category | flops | bytes accessed | tf_op | source)
XLA Modules:
  0.0 525.7 jit_solution(17909985281947806743)
XLA Ops:
  6.5 0.9 select_reduce_fusion.5
  17.3 3.7 select_bitcast_fusion.1
  21.0 1.1 pad_maximum_fusion
  23.2 5.5 %pick.1 = f32[4,1024,256]{2,1,0:T(8,128)} custom-call(s32[4]{0:T(128)} %get-tuple-element.62.idx, s32[4]{0:T(128)} %get-tuple-element.60.loc, f32[1024,1024]{1,0:T(8,128)} %bitcast.172), custom_call_target="tpu_custom_call" | custom-call | tf_op jit(solution)/shard_map/pick/pallas_call | solution.py:33
  28.8 6.5 %all-to-all-start = ((f32[4,1024,256]{2,1,0:T(8,128)}), f32[4,1024,256]{2,1,0:T(8,128)}, u32[]{:S(2)}, u32[]{:S(2)}) async-start(f32[4,1024,256]{2,1,0:T(8,128)} %pick.1), calls=%async_computation | async-start | bytes 8388608 | tf_op jit(solution)/shard_map/all_to_all | solution.py:138
  35.2 0.7 all-gather.2.cloned.1.call-update
  43.6 18.0 %all-reduce.6.cloned.1.call-done.ea.eb = bf16[512,1024]{1,0:T(8,128)(2,1)} async-done(((bf16[512,1024]{1,0:T(8,128)(2,1)}), bf16[512,1024]{1,0:T(8,128)(2,1)}) %all-reduce.6.cloned.1.call-update) | async-done | bytes 1048592 | tf_op jit(solution)/shard_map/psum | solution.py:148
  61.6 5.8 %diag.1 = f32[512,512]{1,0:T(8,128)} custom-call(s32[7,4]{1,0:T(8,128)} %stack.89.t, f32[1024,1024]{1,0:T(8,128)} %bitcast.173, f32[768,1536]{1,0:T(8,128)} %front.5, bf16[512,1024]{1,0:T(8,128)(2,1)} %all-reduce.6.cloned.1.call-done.ea.eb, bf16[512,1024]{1,0:T(8,128)(2,1)} %all-reduce.6.cloned.1.call-done.ea.eb), custom_call_target="tpu_custom_call" | custom-call | tf_op jit(solution)/shard_map/diag/pallas_call | solution.py:33
  67.4 2.5 copy.33
  70.6 15.3 %all-gather.2.cloned.1.call-done.partner = bf16[4,256,1024]{2,1,0:T(8,128)(2,1)} async-done(((bf16[1,256,1024]{2,1,0:T(8,128)(2,1)}), bf16[4,256,1024]{2,1,0:T(8,128)(2,1)}) %all-gather.2.cloned.1.call-update) | async-done | bytes 2097168 | tf_op jit(solution)/shard_map/all_gather | solution.py:149
  85.9 47.8 %all-to-all-done.raw = f32[4,1024,256]{2,1,0:T(8,128)} async-done(((f32[4,1024,256]{2,1,0:T(8,128)}), f32[4,1024,256]{2,1,0:T(8,128)}, u32[]{:S(2)}, u32[]{:S(2)}) %all-to-all-start) | async-done | bytes 4194336 | tf_op jit(solution)/shard_map/all_to_all | solution.py:138
  133.7 15.4 %update.1.upd = f32[4,256,1024]{2,1,0:T(8,128)} custom-call(s32[4]{0:T(128)} %get-tuple-element.64.rows, s32[4,4]{1,0:T(4,128)} %multiply_bitcast_fusion.fac, f32[4,1024,256]{2,1,0:T(8,128)} %all-to-all-done.raw, bf16[1024,1024]{1,0:T(8,128)(2,1)} %bitcast.174, bf16[4,256,1024]{2,1,0:T(8,128)(2,1)} %all-gather.2.cloned.1.call-done.partner), custom_call_target="tpu_custom_call" | custom-call | tf_op jit(solution)/shard_map/update/pallas_call | solution.py:33
  149.1 4.9 all-to-all-start.1
  154.2 1.3 compare_select_fusion.4
  157.5 1.2 stack.88.t
  158.7 0.8 iota_compare_fusion
  159.6 96.7 %all-reduce.8.cloned.1.call-done = f32[512,512]{0,1:T(8,128)} async-done(((f32[512,512]{0,1:T(8,128)}), f32[512,512]{0,1:T(8,128)}) %all-reduce.8.cloned.1.call-update) | async-done | bytes 1048592 | tf_op jit(solution)/shard_map/psum | solution.py:171
  256.3 1.6 copy.34
  257.8 1.4 fusion
  259.3 11.7 %cholesky.104 = f32[128,128]{1,0:T(8,128)S(1)} custom-call(f32[128,128]{1,0:T(8,128)S(1)} %cholesky.266), custom_call_target="Cholesky" | custom-call | tf_op jit(solution)/shard_map/jit(cholesky)/cholesky | solution.py:172
  271.0 9.8 %custom-call.30 = f32[1,128,128]{1,2,0:T(8,128)S(1)} custom-call(f32[1,128,128]{2,1,0:T(8,128)S(1)} %get-tuple-element.47), custom_call_target="InvertDiagBlocksLowerTriangular" | custom-call | tf_op jit(solution)/shard_map/jit(cholesky)/cholesky | solution.py:172
  281.7 11.7 %cholesky.217 = f32[128,128]{1,0:T(8,128)S(1)} custom-call(f32[128,128]{1,0:T(8,128)S(1)} %cholesky.270), custom_call_target="Cholesky" | custom-call | tf_op jit(solution)/shard_map/jit(cholesky)/cholesky | solution.py:172
  293.4 10.2 %custom-call.31 = f32[1,128,128]{1,2,0:T(8,128)S(1)} custom-call(f32[1,128,128]{2,1,0:T(8,128)S(1)} %get-tuple-element.44), custom_call_target="InvertDiagBlocksLowerTriangular" | custom-call | tf_op jit(solution)/shard_map/jit(cholesky)/cholesky | solution.py:172
  304.3 11.7 %cholesky.238 = f32[128,128]{1,0:T(8,128)S(1)} custom-call(f32[128,128]{1,0:T(8,128)S(1)} %cholesky.275), custom_call_target="Cholesky" | custom-call | tf_op jit(solution)/shard_map/jit(cholesky)/cholesky | solution.py:172
  316.0 9.8 %custom-call.32 = f32[1,128,128]{1,2,0:T(8,128)S(1)} custom-call(f32[1,128,128]{2,1,0:T(8,128)S(1)} %get-tuple-element.41), custom_call_target="InvertDiagBlocksLowerTriangular" | custom-call | tf_op jit(solution)/shard_map/jit(cholesky)/cholesky | solution.py:172
  326.4 11.8 %cholesky.255 = f32[128,128]{1,0:T(8,128)S(1)} custom-call(f32[128,128]{1,0:T(8,128)S(1)} %convolution_subtract_fusion.5), custom_call_target="Cholesky" | custom-call | tf_op jit(solution)/shard_map/jit(cholesky)/cholesky | solution.py:172
  339.6 0.7 compare_reduce_fusion.1
  343.6 9.4 %strip.1 = f32[512,1536]{1,0:T(8,128)} custom-call(s32[5,12]{1,0:T(8,128)} %stack.90.t, f32[4,256,1024]{2,1,0:T(8,128)} %update.1.upd, f32[768,1536]{1,0:T(8,128)} %front.5), custom_call_target="tpu_custom_call" | custom-call | tf_op jit(solution)/shard_map/strip/pallas_call | solution.py:33
  353.1 10.5 %while.1 = (s32[]{:T(128)}, f32[512,512]{1,0:T(8,128)S(1)}, s32[4,2]{0,1:T(2,128)S(1)}, f32[4,128,128]{2,1,0:T(8,128)}, s32[]{:T(128)}) while((s32[]{:T(128)}, f32[512,512]{1,0:T(8,128)S(1)}, s32[4,2]{0,1:T(2,128)S(1)}, f32[4,128,128]{2,1,0:T(8,128)}, s32[]{:T(128)}) %tuple.68), condition=%wide.while_cond, body=%wide.while_body.sunk | while | flops 2 | bytes 132205 | solution.py:173
  353.7 2.0 bitcast_dynamic-update-slice_fusion.2
  356.3 2.0 bitcast_dynamic-update-slice_fusion.2
  358.9 2.0 bitcast_dynamic-update-slice_fusion.2
  361.5 2.0 bitcast_dynamic-update-slice_fusion.2
  363.5 40.2 %custom-call.33 = f32[4,128,128]{1,2,0:T(8,128)S(1)} custom-call(f32[4,128,128]{2,1,0:T(8,128)} %get-tuple-element.12), custom_call_target="InvertDiagBlocksLowerTriangular" | custom-call | tf_op jit(solution)/shard_map/triangular_solve | solution.py:173
  403.7 1.2 fusion.13
  404.9 1.1 convolution_subtract_fusion.1
  406.0 16.2 %all-reduce.10.cloned.1.call-done = f32[512,1536]{1,0:T(8,128)} async-done(((f32[512,1536]{1,0:T(8,128)}), f32[512,1536]{1,0:T(8,128)}) %all-reduce.10.cloned.1.call-update) | async-done | bytes 3145744 | tf_op jit(solution)/shard_map/psum | solution.py:212
  422.2 2.7 dynamic-slice_select_fusion
  424.9 1.6 fusion.25
  426.5 1.5 convolution_subtract_fusion
  428.0 1.3 fusion.23
  429.3 1.8 convolution_subtract_fusion.2
  431.1 1.3 fusion.22
  432.4 0.7 copy-done.7
  433.1 6.9 %fusion.6.wc = f32[512,1536]{1,0:T(8,128)} fusion(f32[512,1536]{1,0:T(8,128)S(1)} %copy-done.2, f32[128,512]{1,0:T(8,128)S(1)} %fusion.22, f32[128,512]{1,0:T(8,128)S(1)} %fusion.23, f32[128,512]{1,0:T(8,128)S(1)} %fusion.25, f32[128,512]{1,0:T(8,128)S(1)} %fusion.13), kind=kOutput, calls=%fused_computation.31 | convolution fusion | flops 4832624640 | bytes 7340032 | tf_op jit(solution)/shard_map/dot_general | solution.py:215
  440.0 53.9 %all-reduce.12.cloned.1.call-done = f32[512,768]{1,0:T(8,128)} async-done(((f32[512,768]{1,0:T(8,128)}), f32[512,768]{1,0:T(8,128)}) %all-reduce.12.cloned.1.call-update) | async-done | bytes 1572880 | tf_op jit(solution)/shard_map/psum | solution.py:214
  493.9 5.5 %fusion.7.wr = f32[512,768]{1,0:T(8,128)} fusion(f32[512,768]{1,0:T(8,128)} %all-reduce.12.cloned.1.call-done, f32[128,512]{1,0:T(8,128)} %copy-done.7, f32[128,512]{1,0:T(8,128)} %copy-done.4, f32[128,512]{1,0:T(8,128)} %copy-done.3, f32[128,512]{1,0:T(8,128)S(1)} %fusion.13), kind=kOutput, calls=%fused_computation.32 | convolution fusion | flops 2416705536 | bytes 4194304 | tf_op jit(solution)/shard_map/dot_general | solution.py:216
  499.4 19.6 %final.1 = f32[768,1536]{1,0:T(8,128)} custom-call(s32[13,18]{1,0:T(8,128)} %stack.88.t, f32[768,1536]{1,0:T(8,128)} %front.5, f32[4,256,1024]{2,1,0:T(8,128)} %all-to-all-done.1.a0.a1, f32[4,256,1024]{2,1,0:T(8,128)} %collective-permute-done.b0.b1, f32[4,256,1024]{2,1,0:T(8,128)} %all-to-all-done.1.a0.a1, f32[4,256,1024]{2,1,0:T(8,128)} %collective-permute-done.b0.b1, ...), custom_call_target="tpu_custom_call" | custom-call | tf_op jit(solution)/shard_map/final/pallas_call | solution.py:33
  (155 shorter events, 23.5 us)
Async XLA Ops:
  6.5 32.2 %copy-start = (s32[2,16,16]{2,1,0:T(8,128)S(1)}, s32[2,16,16]{2,1,0:T(8,128)}, u32[]{:S(2)}) copy-start(s32[2,16,16]{2,1,0:T(8,128)} %param.10) | copy-start | bytes 6148
  6.5 55.0 %all-reduce.6.cloned.1.call-start = ((), (), s32[]{:S(2)}) async-start(), calls=%async_computation.3 | async-start | bytes 2097152 | tf_op jit(solution)/shard_map/psum | solution.py:148
  28.8 7.3 %copy-start.11 = (s32[4]{0:T(128)S(1)}, s32[4]{0:T(128)}, u32[]{:S(2)}) copy-start(s32[4]{0:T(128)} %constant.467) | copy-start | bytes 52
  28.8 8.6 %copy-start.10 = (s32[4]{0:T(128)S(1)}, s32[4]{0:T(128)}, u32[]{:S(2)}) copy-start(s32[4]{0:T(128)} %constant.466) | copy-start | bytes 52
  28.8 104.9 %all-to-all-start = ((f32[4,1024,256]{2,1,0:T(8,128)}), f32[4,1024,256]{2,1,0:T(8,128)}, u32[]{:S(2)}, u32[]{:S(2)}) async-start(f32[4,1024,256]{2,1,0:T(8,128)} %pick.1), calls=%async_computation | async-start | bytes 8388608 | tf_op jit(solution)/shard_map/all_to_all | solution.py:138
  35.2 50.7 %all-gather.2.cloned.1.call-start = ((), (), s32[]{:S(2)}) async-start(), calls=%async_computation.2 | async-start | bytes 2621440 | tf_op jit(solution)/shard_map/all_gather | solution.py:149
  36.0 220.3 %all-reduce.8.cloned.1.call-start = ((), (), s32[]{:S(2)}) async-start(), calls=%async_computation.4 | async-start | bytes 2097152 | tf_op jit(solution)/shard_map/psum | solution.py:171
  67.4 2.6 copy-start.9
  149.1 191.3 %all-to-all-start.1 = ((f32[4,256,1024]{2,1,0:T(8,128)}), f32[4,256,1024]{2,1,0:T(8,128)}, u32[]{:S(2)}, u32[]{:S(2)}) async-start(f32[4,256,1024]{2,1,0:T(8,128)} %update.1.upd), calls=%async_computation.1 | async-start | bytes 8388608 | tf_op jit(solution)/shard_map/all_to_all | solution.py:189
  153.9 268.3 %all-reduce.10.cloned.1.call-start = ((), (), s32[]{:S(2)}) async-start(), calls=%async_computation.5 | async-start | bytes 6291456 | tf_op jit(solution)/shard_map/psum | solution.py:212
  159.6 245.3 %copy-start.5 = (f32[512,512]{1,0:T(8,128)}, f32[512,512]{1,0:T(8,128)S(1)}, u32[]{:S(2)}) copy-start(f32[512,512]{1,0:T(8,128)S(1)} %fusion.11) | copy-start | bytes 3145732
  340.3 159.1 %collective-permute-start = (f32[4,256,1024]{2,1,0:T(8,128)}, f32[4,256,1024]{2,1,0:T(8,128)}, u32[]{:S(2)}, u32[]{:S(2)}) collective-permute-start(f32[4,256,1024]{2,1,0:T(8,128)} %all-to-all-done.1.a0.a1), channel_id=1, source_target_pairs={{0,4},{4,0},{1,5},{5,1},{2,6},{6,2},{3,7},{7,3},{8,12},{12,8},{9,1... | collective-permute-start | bytes 12582920 | tf_op jit(solution)/shard_map/ppermute | solution.py:190
  353.0 140.9 %all-reduce.12.cloned.1.call-start = ((), (), s32[]{:S(2)}) async-start(), calls=%async_computation.6 | async-start | bytes 3145728 | tf_op jit(solution)/shard_map/psum | solution.py:214
  363.5 58.7 %copy-start.6 = (f32[512,512]{1,0:T(8,128)}, f32[512,512]{1,0:T(8,128)S(1)}, u32[]{:S(2)}) copy-start(f32[512,512]{1,0:T(8,128)S(1)} %get-tuple-element.166) | copy-start | bytes 3145732
  403.7 18.5 %copy-start.8 = (f32[4,128,128]{1,2,0:T(8,128)}, f32[4,128,128]{1,2,0:T(8,128)S(1)}, u32[]{:S(2)}) copy-start(f32[4,128,128]{1,2,0:T(8,128)S(1)} %custom-call.33) | copy-start | bytes 786436
  424.9 8.3 %copy-start.2 = (f32[512,1536]{1,0:T(8,128)S(1)}, f32[512,1536]{1,0:T(8,128)}, u32[]{:S(2)}) copy-start(f32[512,1536]{1,0:T(8,128)} %all-reduce.10.cloned.1.call-done) | copy-start | bytes 9437188
  426.4 5.9 %copy-start.3 = (f32[128,512]{1,0:T(8,128)}, f32[128,512]{1,0:T(8,128)S(1)}, u32[]{:S(2)}) copy-start(f32[128,512]{1,0:T(8,128)S(1)} %fusion.25) | copy-start | bytes 786436
  429.3 3.1 copy-start.4
  432.4 0.7 copy-start.7
  499.4 19.6 %copy-start.1 = (s32[2,16,16]{2,1,0:T(8,128)S(1)}, s32[2,16,16]{2,1,0:T(8,128)}, u32[]{:S(2)}) copy-start(s32[2,16,16]{2,1,0:T(8,128)} %param.10) | copy-start | bytes 6148
Sparse Core Ops, SparseCore 0:
  22.2 39.3 all-reduce.5
  63.1 22.7 all-gather.1
  91.1 165.1 all-reduce.7
  353.1 69.0 all-reduce.9
  425.0 68.8 all-reduce.11

commit v2 on v1

--- a/solution.py
+++ b/solution.py
@@ -83,6 +83,74 @@
     @pl.when(panel == 2)
     def _():
         out[...] = wr[TILE:, :].T
+
+
+BASE = 128
+WIDE = 2
+
+
+def base_inverse(a_ref, d_ref, x_ref):
+    n, step = a_ref.shape[0], 8
+    ids = lax.broadcasted_iota(jnp.int32, (step, n), 0)
+    lanes = lax.broadcasted_iota(jnp.int32, (step, n), 1)
+    a = [a_ref[i * step : (i + 1) * step, :] for i in range(n // step)]
+    x = [(lanes == ids + i * step).astype(F32) for i in range(n // step)]
+    for j in range(0, n, WIDE):
+        c0 = j // step
+        chunks = range(c0, n // step)
+        cols = [[jnp.broadcast_to(a[i][:, j + t : j + t + 1], (step, n)) for i in chunks] for t in range(WIDE)]
+        at = [j + t - c0 * step for t in range(WIDE)]
+        rows = [a[c0][p : p + 1, :] for p in at]
+        xrows = [x[c0][p : p + 1, :] for p in at]
+        for t in range(WIDE):
+            pivot = cols[t][0][at[t] : at[t] + 1, :]
+            d_ref[j + t : j + t + 1, :] = pivot
+            inv = 1.0 / pivot
+            low = [c * inv for c in cols[t]]
+            low[0] = jnp.where(ids > at[t], low[0], 0.0)
+            for s in range(t + 1, WIDE):
+                f = cols[t][0][at[s] : at[s] + 1, :]
+                g = f * inv
+                cols[s] = [c - l * f for c, l in zip(cols[s], low)]
+                rows[s] = rows[s] - g * rows[t]
+                xrows[s] = xrows[s] - g * xrows[t]
+            for n_, i in enumerate(chunks):
+                a[i] = a[i] - low[n_] * rows[t]
+                x[i] = x[i] - low[n_] * xrows[t]
+    for i in range(n // step):
+        x_ref[i * step : (i + 1) * step, :] = x[i] * (1.0 / jnp.sqrt(d_ref[i * step : (i + 1) * step, :]))
+
+
+def factor_kernel(a_in, y, a, blk, piv, inv):
+    n = a.shape[0]
+    high = functools.partial(lax.dot_general, precision=lax.Precision.HIGHEST, preferred_element_type=F32)
+    ids = lax.broadcasted_iota(jnp.int32, (n, n), 0)
+    a[...] = a_in[...]
+    y[...] = (ids == lax.broadcasted_iota(jnp.int32, (n, n), 1)).astype(F32)
+
+    def one(k, carry):
+        at = pl.ds(pl.multiple_of(k * BASE, BASE), BASE)
+        blk[...] = a[at, at]
+        base_inverse(blk, piv, inv)
+        low = high(a[:, at], inv[...], NT)
+        low = jnp.where(ids[:, :BASE] >= (k + 1) * BASE, low, 0.0)
+        yk = high(inv[...], y[at, :], (((1,), (0,)), ((), ())))
+        a[...] = a[...] - high(low, low, NT)
+        y[...] = y[...] - high(low, yk, (((1,), (0,)), ((), ())))
+        y[at, :] = yk
+        return carry
+
+    lax.fori_loop(0, n // BASE, one, 0)
+
+
+def factor_inverse(d):
+    n = d.shape[0]
+    return pl.pallas_call(
+        factor_kernel,
+        out_shape=jax.ShapeDtypeStruct(d.shape, F32),
+        scratch_shapes=[pltpu.VMEM((n, n), F32)] + [pltpu.VMEM((BASE, BASE), F32)] * 3,
+        name="factor",
+    )(d)
 
 
 def body(child_blocks, child_panels, child_patterns, child_maps, parent_place, parent_front):
@@ -169,10 +237,7 @@
         pl.BlockSpec((TILE, TILE), lambda a, b, t: (a, b)), "diag",
     )
     diagonal = lax.psum(diag_part, ("child", "rx", "core", "col"))
-    factor = jnp.linalg.cholesky(diagonal)
-    inverse = lax.linalg.triangular_solve(
-        factor, jnp.eye(2 * TILE, dtype=F32), left_side=True, lower=True
-    )
+    inverse = factor_inverse(diagonal)
 
     col_ids = jnp.arange(blocks, dtype=i32) * td + in_tile
     factors = pat[row * td + row_tile][:, col_ids] * row_ok[:, None] * in_ok[None, :]

time: 531 us -> 500 us (0.942)
  other arithmetic: 136 us -> 11.2 us
  waiting for transfers between devices: 249 us -> 329 us
  Pallas kernels: 55.7 us -> 101 us
  local copies, waits for them, and re-layouts: 28.6 us -> 13.3 us
  matrix products: 24 us -> 14 us
    another operation x18 -> x0, other arithmetic: 120 us -> none  [the longest x15 79.6 us: body(): factor = jnp.linalg.cholesky(diagonal)]
    all_to_all x1, waiting for transfers between devices: 0.01 us -> 51.5 us  [body(): lax.all_to_all(update, ('child', 'rx'), split_axis=0, concat_axis=0, tile...]
    pallas_call x0 -> x1, Pallas kernels: none -> 46 us  [factor_inverse(): pl.pallas_call(factor_kernel, out_shape=jax.ShapeDtypeStruct(d.shape, F32...]
    psum x1, waiting for transfers between devices: 53.9 us -> 15.5 us  [body(): half = lax.psum(jnp.where(chip == col, half, jnp.zeros_like(half)), 'col')]
    psum x1, waiting for transfers between devices: 16.2 us -> 50.7 us  [body(): strip = lax.psum(strip_part, ('child', 'rx', 'core'))]
    psum x1, waiting for transfers between devices: 96.7 us -> 131 us  [body(): diagonal = lax.psum(diag_part, ('child', 'rx', 'core', 'col'))]
    psum x1, waiting for transfers between devices: 18 us -> 0.01 us  [body(): e_all = lax.psum(e_rows, ('rx', 'core'))]
    another operation x13 -> x0, matrix products: 11.6 us -> none  [the longest x7 9.69 us: body(): lax.linalg.triangular_solve(factor, jnp.eye(2 * TILE, dtype=F32), left_si...]
  transfers between devices with their start and end apart: 8 -> 8, of which waited for: 6 -> 6; matrix products, arithmetic and copies ran while one was open for 34% -> 7% of each run, Pallas kernels for 7% -> 12%
where the time goes in v2:
time: 500 us; the launch traced here: 499 us
  waiting for transfers between devices  329 us (66%)
  Pallas kernels  101 us (20%)
  between operations  18.4 us (4%)
  matrix products  14 us (3%)
  local copies, waits for them, and re-layouts  13.3 us (3%)
  starting transfers between devices  11.7 us (2%)
  other arithmetic  11.2 us (2%)
    psum x1, waiting for transfers between devices, body(): diagonal = lax.psum(diag_part, ('child', 'rx', 'core', 'col'))  131 us
    all_to_all x1, waiting for transfers between devices, body(): lax.all_to_all(outgoing, 'col', split_axis=0, concat_axis=0, tiled=True)  58.6 us
    pallas_call x5, Pallas kernels, tile_call(): pl.pallas_call(kernel, grid_spec=pltpu.PrefetchScalarGridSpec(num_scalar_...  55.3 us
    all_to_all x1, waiting for transfers between devices, body(): lax.all_to_all(update, ('child', 'rx'), split_axis=0, concat_axis=0, tile...  51.5 us
    psum x1, waiting for transfers between devices, body(): strip = lax.psum(strip_part, ('child', 'rx', 'core'))  50.7 us
    pallas_call x1, Pallas kernels, factor_inverse(): pl.pallas_call(factor_kernel, out_shape=jax.ShapeDtypeStruct(d.shape, F32...  46 us
    all_gather x1, waiting for transfers between devices, body(): partner = lax.all_gather(part, ('rx', 'core'), axis=0)  21.6 us
    psum x1, waiting for transfers between devices, body(): half = lax.psum(jnp.where(chip == col, half, jnp.zeros_like(half)), 'col')  15.5 us
  transfers between devices with their start and end apart: 8, of which 6 were waited for; matrix products, arithmetic and copies ran while one was open for 7% of the time, Pallas kernels for 12%

profile of v2, /device:TPU:0, one launch (start us, length us, event | category | flops | bytes accessed | tf_op | source)
XLA Modules:
  0.0 498.5 jit_solution(8695339121093225790)
XLA Ops:
  6.5 0.9 select_reduce_fusion.1
  7.7 0.2 fusion
  7.8 0.2 select_reduce_fusion.2
  8.0 0.6 fusion.13
  8.6 0.6 fusion.12
  9.1 5.5 %pick.1 = f32[4,1024,256]{2,1,0:T(8,128)} custom-call(s32[4]{0:T(128)} %get-tuple-element.34.idx, s32[4]{0:T(128)} %get-tuple-element.32.loc, f32[1024,1024]{1,0:T(8,128)} %bitcast.126), custom_call_target="tpu_custom_call" | custom-call | tf_op jit(solution)/shard_map/pick/pallas_call | solution.py:33
  14.7 6.5 %all-to-all-start = ((f32[4,1024,256]{2,1,0:T(8,128)}), f32[4,1024,256]{2,1,0:T(8,128)}, u32[]{:S(2)}, u32[]{:S(2)}) async-start(f32[4,1024,256]{2,1,0:T(8,128)} %pick.1), calls=%async_computation | async-start | bytes 8388608 | tf_op jit(solution)/shard_map/all_to_all | solution.py:206
  21.2 0.6 dynamic_slice.71
  21.7 0.6 dynamic_slice.70
  22.5 0.6 gather_fusion.2
  23.1 0.6 fusion.25
  28.7 0.6 fusion.24
  29.4 2.4 select_bitcast_fusion.1
  31.8 0.2 fusion.6
  32.0 0.1 copy.20
  32.1 0.1 fusion.7
  32.2 0.6 gather_fusion
  32.9 0.2 fusion.8
  33.1 0.6 gather_fusion.1
  33.6 0.1 copy.24
  33.7 0.7 multiply_bitcast_fusion.fac
  34.4 21.6 %all-gather.2.cloned.1.call-done.partner = bf16[4,256,1024]{2,1,0:T(8,128)(2,1)} async-done(((bf16[1,256,1024]{2,1,0:T(8,128)(2,1)}), bf16[4,256,1024]{2,1,0:T(8,128)(2,1)}) %all-gather.2.cloned.1.call-update) | async-done | bytes 2097168 | tf_op jit(solution)/shard_map/all_gather | solution.py:217
  56.0 58.6 %all-to-all-done.raw = f32[4,1024,256]{2,1,0:T(8,128)} async-done(((f32[4,1024,256]{2,1,0:T(8,128)}), f32[4,1024,256]{2,1,0:T(8,128)}, u32[]{:S(2)}, u32[]{:S(2)}) %all-to-all-start) | async-done | bytes 4194336 | tf_op jit(solution)/shard_map/all_to_all | solution.py:206
  114.6 15.4 %update.1.upd = f32[4,256,1024]{2,1,0:T(8,128)} custom-call(s32[4]{0:T(128)} %get-tuple-element.36.rows, s32[4,4]{1,0:T(4,128)} %multiply_bitcast_fusion.fac, f32[4,1024,256]{2,1,0:T(8,128)} %all-to-all-done.raw, bf16[1024,1024]{1,0:T(8,128)(2,1)} %bitcast.128, bf16[4,256,1024]{2,1,0:T(8,128)(2,1)} %all-gather.2.cloned.1.call-done.partner), custom_call_target="tpu_custom_call" | custom-call | tf_op jit(solution)/shard_map/update/pallas_call | solution.py:33
  130.0 4.8 all-to-all-start.1
  134.9 1.0 pad_maximum_fusion
  137.0 0.6 stack.90.t
  137.6 9.4 %strip.1 = f32[512,1536]{1,0:T(8,128)} custom-call(s32[5,12]{1,0:T(8,128)} %stack.90.t, f32[4,256,1024]{2,1,0:T(8,128)} %update.1.upd, f32[768,1536]{1,0:T(8,128)} %front.5), custom_call_target="tpu_custom_call" | custom-call | tf_op jit(solution)/shard_map/strip/pallas_call | solution.py:33
  147.1 51.5 %all-to-all-done.1.a0.a1 = f32[4,256,1024]{2,1,0:T(8,128)} async-done(((f32[4,256,1024]{2,1,0:T(8,128)}), f32[4,256,1024]{2,1,0:T(8,128)}, u32[]{:S(2)}, u32[]{:S(2)}) %all-to-all-start.1) | async-done | bytes 4194336 | tf_op jit(solution)/shard_map/all_to_all | solution.py:254
  198.6 0.6 gather_fusion.4
  199.2 0.6 gather_fusion.6
  199.8 0.6 gather_fusion.5
  200.5 0.6 gather_fusion.3
  201.1 0.6 gather_fusion.7
  201.8 0.6 stack.89.t
  202.6 0.6 fusion.26
  203.2 5.9 %diag.1 = f32[512,512]{1,0:T(8,128)} custom-call(s32[7,4]{1,0:T(8,128)} %stack.89.t, f32[1024,1024]{1,0:T(8,128)} %bitcast.127, f32[768,1536]{1,0:T(8,128)} %front.5, bf16[512,1024]{1,0:T(8,128)(2,1)} %all-reduce.5.cloned.1.call-done.ea.eb, bf16[512,1024]{1,0:T(8,128)(2,1)} %all-reduce.5.cloned.1.call-done.ea.eb), custom_call_target="tpu_custom_call" | custom-call | tf_op jit(solution)/shard_map/diag/pallas_call | solution.py:33
  209.1 0.2 all-reduce.11.cloned.1.call-start
  209.3 1.2 compare_select_fusion.4
  210.8 50.7 %all-reduce.9.cloned.1.call-done = f32[512,1536]{1,0:T(8,128)} async-done(((f32[512,1536]{1,0:T(8,128)}), f32[512,1536]{1,0:T(8,128)}) %all-reduce.9.cloned.1.call-update) | async-done | bytes 3145744 | tf_op jit(solution)/shard_map/psum | solution.py:277
  261.6 2.7 dynamic-slice_select_fusion
  265.4 1.2 stack.88.t
  266.7 130.7 %all-reduce.7.cloned.1.call-done.a_in = f32[512,512]{1,0:T(8,128)} async-done(((f32[512,512]{1,0:T(8,128)}), f32[512,512]{1,0:T(8,128)}) %all-reduce.7.cloned.1.call-update) | async-done | bytes 1048592 | tf_op jit(solution)/shard_map/psum | solution.py:239
  397.4 46.0 %factor.1 = f32[512,512]{1,0:T(8,128)} custom-call(f32[512,512]{1,0:T(8,128)} %all-reduce.7.cloned.1.call-done.a_in), custom_call_target="tpu_custom_call" | custom-call | tf_op jit(solution)/shard_map/factor/pallas_call | solution.py:148
  443.4 8.7 %fusion.28.wc = f32[512,1536]{1,0:T(8,128)} fusion(f32[512,512]{1,0:T(8,128)} %factor.1, f32[512,1536]{1,0:T(8,128)} %all-reduce.9.cloned.1.call-done), kind=kOutput, calls=%fused_computation.152 | convolution fusion | flops 4831838208 | bytes 7340032 | tf_op jit(solution)/shard_map/dot_general | solution.py:280
  452.1 15.5 %all-reduce.11.cloned.1.call-done = f32[512,768]{1,0:T(8,128)} async-done(((f32[512,768]{1,0:T(8,128)}), f32[512,768]{1,0:T(8,128)}) %all-reduce.11.cloned.1.call-update) | async-done | bytes 1572880 | tf_op jit(solution)/shard_map/psum | solution.py:279
  467.6 5.3 %fusion.27.wr = f32[512,768]{1,0:T(8,128)} fusion(f32[512,512]{1,0:T(8,128)S(1)} %copy-done.1, f32[512,768]{1,0:T(8,128)} %all-reduce.11.cloned.1.call-done), kind=kOutput, calls=%fused_computation.151 | convolution fusion | flops 2415919104 | bytes 4194304 | tf_op jit(solution)/shard_map/dot_general | solution.py:281
  472.9 19.1 %final.1 = f32[768,1536]{1,0:T(8,128)} custom-call(s32[13,18]{1,0:T(8,128)} %stack.88.t, f32[768,1536]{1,0:T(8,128)} %front.5, f32[4,256,1024]{2,1,0:T(8,128)} %all-to-all-done.1.a0.a1, f32[4,256,1024]{2,1,0:T(8,128)} %collective-permute-done.b0.b1, f32[4,256,1024]{2,1,0:T(8,128)} %all-to-all-done.1.a0.a1, f32[4,256,1024]{2,1,0:T(8,128)} %collective-permute-done.b0.b1, ...), custom_call_target="tpu_custom_call" | custom-call | tf_op jit(solution)/shard_map/final/pallas_call | solution.py:33
  (90 shorter events, 3.3 us)
Async XLA Ops:
  6.5 25.7 %copy-start = (s32[2,16,16]{2,1,0:T(8,128)S(1)}, s32[2,16,16]{2,1,0:T(8,128)}, u32[]{:S(2)}) copy-start(s32[2,16,16]{2,1,0:T(8,128)} %param.10) | copy-start | bytes 6148
  14.7 7.8 %copy-start.3 = (s32[24]{0:T(128)S(1)}, s32[24]{0:T(128)}, u32[]{:S(2)}) copy-start(s32[24]{0:T(128)} %param.12) | copy-start | bytes 292
  14.7 14.7 %copy-start.2 = (bf16[1,1024,1024]{2,1,0:T(8,128)(2,1)S(1)}, bf16[1,1024,1024]{2,1,0:T(8,128)(2,1)}, u32[]{:S(2)}) copy-start(bf16[1,1024,1024]{2,1,0:T(8,128)(2,1)} %param.9) | copy-start | bytes 6291460
  14.7 99.9 %all-to-all-start = ((f32[4,1024,256]{2,1,0:T(8,128)}), f32[4,1024,256]{2,1,0:T(8,128)}, u32[]{:S(2)}, u32[]{:S(2)}) async-start(f32[4,1024,256]{2,1,0:T(8,128)} %pick.1), calls=%async_computation | async-start | bytes 8388608 | tf_op jit(solution)/shard_map/all_to_all | solution.py:206
  21.2 34.8 %all-gather.2.cloned.1.call-start = ((), (), s32[]{:S(2)}) async-start(), calls=%async_computation.2 | async-start | bytes 2621440 | tf_op jit(solution)/shard_map/all_gather | solution.py:217
  130.0 68.6 %all-to-all-start.1 = ((f32[4,256,1024]{2,1,0:T(8,128)}), f32[4,256,1024]{2,1,0:T(8,128)}, u32[]{:S(2)}, u32[]{:S(2)}) async-start(f32[4,256,1024]{2,1,0:T(8,128)} %update.1.upd), calls=%async_computation.1 | async-start | bytes 8388608 | tf_op jit(solution)/shard_map/all_to_all | solution.py:254
  134.8 2.8 copy-start.5
  134.8 68.4 %all-reduce.5.cloned.1.call-start = ((), (), s32[]{:S(2)}) async-start(), calls=%async_computation.3 | async-start | bytes 2097152 | tf_op jit(solution)/shard_map/psum | solution.py:216
  136.0 125.6 %all-reduce.9.cloned.1.call-start = ((), (), s32[]{:S(2)}) async-start(), calls=%async_computation.5 | async-start | bytes 6291456 | tf_op jit(solution)/shard_map/psum | solution.py:277
  147.0 51.6 %copy-start.4 = (s32[4]{0:T(128)S(1)}, s32[4]{0:T(128)}, u32[]{:S(2)}) copy-start(s32[4]{0:T(128)} %constant.312) | copy-start | bytes 52
  147.0 250.3 %all-reduce.7.cloned.1.call-start = ((), (), s32[]{:S(2)}) async-start(), calls=%async_computation.4 | async-start | bytes 2097152 | tf_op jit(solution)/shard_map/psum | solution.py:239
  198.5 274.4 %collective-permute-start = (f32[4,256,1024]{2,1,0:T(8,128)}, f32[4,256,1024]{2,1,0:T(8,128)}, u32[]{:S(2)}, u32[]{:S(2)}) collective-permute-start(f32[4,256,1024]{2,1,0:T(8,128)} %all-to-all-done.1.a0.a1), channel_id=1, source_target_pairs={{0,4},{4,0},{1,5},{5,1},{2,6},{6,2},{3,7},{7,3},{8,12},{12,8},{9,1... | collective-permute-start | bytes 12582920 | tf_op jit(solution)/shard_map/ppermute | solution.py:255
  209.1 258.5 %all-reduce.11.cloned.1.call-start = ((), (), s32[]{:S(2)}) async-start(), calls=%async_computation.6 | async-start | bytes 3145728 | tf_op jit(solution)/shard_map/psum | solution.py:279
  443.4 24.2 %copy-start.1 = (f32[512,512]{1,0:T(8,128)S(1)}, f32[512,512]{1,0:T(8,128)}, u32[]{:S(2)}) copy-start(f32[512,512]{1,0:T(8,128)} %factor.1) | copy-start | bytes 3145732
Sparse Core Ops, SparseCore 0:
  31.9 24.0 all-gather.1
  138.0 50.8 all-reduce.4
  192.2 69.3 all-reduce.8
  266.6 130.7 all-reduce.6
  399.6 67.9 all-reduce.10

commit v3 on v2

--- a/solution.py
+++ b/solution.py
@@ -50,7 +50,7 @@
 def diag_kernel(t, blk, front, ea, eb, out):
     k = pl.program_id(0) * 2 + pl.program_id(1)
     x = jnp.where(t[4, k] != 0, blk[...], 0.0) + jnp.where(t[5, k] != 0, front[...], 0.0)
-    out[...] = x - jnp.where(t[6, k] != 0, dot(ea[...], eb[...], NT), 0.0)
+    out[...] = x - jnp.where(t[6, k] != 0, dot(ea[...], eb[0], NT), 0.0)
 
 
 def update_kernel(rows, fac, raw, panel, partner, out):
@@ -86,6 +86,7 @@
 
 
 BASE = 128
+FACTOR_WORK = 40_000_000_000
 WIDE = 2
 
 
@@ -150,6 +151,7 @@
         out_shape=jax.ShapeDtypeStruct(d.shape, F32),
         scratch_shapes=[pltpu.VMEM((n, n), F32)] + [pltpu.VMEM((BASE, BASE), F32)] * 3,
         name="factor",
+        cost_estimate=pl.CostEstimate(flops=FACTOR_WORK, bytes_accessed=8 * n * n, transcendentals=0),
     )(d)
 
 
@@ -209,11 +211,6 @@
     part = jnp.where(row_ok[col] != 0, part, jnp.zeros_like(part))
 
     e_here = jnp.logical_and(ie >= 0, ie // td == row)
-    e_rows = jnp.concatenate([
-        jnp.where(e_here[a], lax.dynamic_slice(own, ((ie[a] % td) * TILE, 0), (TILE, depth)), jnp.zeros((), BF16))
-        for a in range(2)
-    ])
-    e_all = lax.psum(e_rows, ("rx", "core"))
     partner = lax.all_gather(part, ("rx", "core"), axis=0)
     pair_a = jnp.array([0, 0, 1, 1], i32)
     pair_b = jnp.array([0, 1, 0, 1], i32)
@@ -223,20 +220,22 @@
         jnp.maximum(ia, 0) % td, jnp.maximum(ib, 0) % td, ea % rd, eb % cd,
         live & (ia // td == row) & (ib // td == col),
         (ea // rd == group) & (eb // cd == col),
-        live & (row == 0) & (col == 0),
+        live & (ia // td == row) & (eb // cd == col), jnp.maximum(ib, 0) // td,
     ]).astype(i32)
     diag_part = tile_call(
-        diag_kernel, (2, 2), (table,), (block, parent_front, e_all, e_all),
+        diag_kernel, (2, 2), (table,), (block, parent_front, own, partner),
         [
             pl.BlockSpec((TILE, TILE), lambda a, b, t: (t[0, a * 2 + b], t[1, a * 2 + b])),
             pl.BlockSpec((TILE, TILE), lambda a, b, t: (t[2, a * 2 + b], t[3, a * 2 + b])),
-            pl.BlockSpec((TILE, depth), lambda a, b, t: (a, 0)),
-            pl.BlockSpec((TILE, depth), lambda a, b, t: (b, 0)),
+            pl.BlockSpec((TILE, depth), lambda a, b, t: (t[0, a * 2 + b], 0)),
+            pl.BlockSpec((1, TILE, depth), lambda a, b, t: (t[7, a * 2 + b], 0, 0)),
         ],
         jax.ShapeDtypeStruct((2 * TILE, 2 * TILE), F32),
         pl.BlockSpec((TILE, TILE), lambda a, b, t: (a, b)), "diag",
     )
-    diagonal = lax.psum(diag_part, ("child", "rx", "core", "col"))
+    plane = ("child", "rx", "core")
+    diagonal = lax.psum_scatter(diag_part, plane, scatter_dimension=0, tiled=True)
+    diagonal = lax.all_gather(lax.psum(diagonal, "col"), plane, axis=0, tiled=True)
     inverse = factor_inverse(diagonal)
 
     col_ids = jnp.arange(blocks, dtype=i32) * td + in_tile
@@ -274,9 +273,13 @@
         jax.ShapeDtypeStruct((2 * TILE, cd * TILE), F32),
         pl.BlockSpec((TILE, TILE), lambda a, q, t: (a, q)), "strip",
     )
-    strip = lax.psum(strip_part, ("child", "rx", "core"))
-    half = lax.dynamic_slice(strip, (0, core * rd * TILE), (2 * TILE, rd * TILE))
-    half = lax.psum(jnp.where(chip == col, half, jnp.zeros_like(half)), "col")
+    piece = lax.psum_scatter(strip_part, plane, scatter_dimension=0, tiled=True)
+    pieces = lax.all_gather(piece, "col", axis=0)
+    strip = lax.all_gather(piece, plane, axis=0, tiled=True)
+    pieces = pieces.reshape(chips, piece.shape[0], cores, rd * TILE).transpose(0, 2, 1, 3)
+    pieces = pieces.reshape(chips * cores, piece.shape[0], rd * TILE)
+    half = lax.all_to_all(pieces, plane, split_axis=0, concat_axis=0, tiled=True)
+    half = half.reshape(2 * TILE, rd * TILE)
     wc = lax.dot_general(inverse, strip, (((1,), (0,)), ((), ())), precision=lax.Precision.HIGHEST)
     wr = lax.dot_general(inverse, half, (((1,), (0,)), ((), ())), precision=lax.Precision.HIGHEST)
 

time: 500 us -> 377 us (0.75)
  waiting for transfers between devices: 329 us -> 208 us
    psum x4 -> x1, waiting for transfers between devices: 197 us -> 31.9 us  [body(): lax.psum(diagonal, 'col')]
    all_gather x0 -> x3, waiting for transfers between devices: none -> 45.5 us  [the longest x1 22.9 us: body(): lax.all_gather(lax.psum(diagonal, 'col'), plane, axis=0, tiled=True)]
    reduce_scatter x0 -> x2, waiting for transfers between devices: none -> 44.8 us  [the longest x1 44.8 us: body(): piece = lax.psum_scatter(strip_part, plane, scatter_dimension=0, tiled=True)]
    all_to_all x1, waiting for transfers between devices: 51.5 us -> 12.5 us  [body(): lax.all_to_all(update, ('child', 'rx'), split_axis=0, concat_axis=0, tile...]
  transfers between devices with their start and end apart: 8 -> 11, of which waited for: 6 -> 7; matrix products, arithmetic and copies ran while one was open for 7% -> 9% of each run, Pallas kernels for 12% -> 20%
where the time goes in v3:
time: 377 us; the launch traced here: 375 us
  waiting for transfers between devices  208 us (55%)
  Pallas kernels  101 us (27%)
  starting transfers between devices  15.4 us (4%)
  between operations  15 us (4%)
  local copies, waits for them, and re-layouts  13.7 us (4%)
  matrix products  13.3 us (4%)
  other arithmetic  8.18 us (2%)
    all_to_all x1, waiting for transfers between devices, body(): lax.all_to_all(outgoing, 'col', split_axis=0, concat_axis=0, tiled=True)  55.7 us
    pallas_call x5, Pallas kernels, tile_call(): pl.pallas_call(kernel, grid_spec=pltpu.PrefetchScalarGridSpec(num_scalar_...  55 us
    pallas_call x1, Pallas kernels, factor_inverse(): pl.pallas_call(factor_kernel, out_shape=jax.ShapeDtypeStruct(d.shape, F32...  46 us
    reduce_scatter x1, waiting for transfers between devices, body(): piece = lax.psum_scatter(strip_part, plane, scatter_dimension=0, tiled=True)  44.8 us
    psum x1, waiting for transfers between devices, body(): lax.psum(diagonal, 'col')  31.9 us
    all_gather x1, waiting for transfers between devices, body(): lax.all_gather(lax.psum(diagonal, 'col'), plane, axis=0, tiled=True)  22.9 us
    all_gather x1, waiting for transfers between devices, body(): pieces = lax.all_gather(piece, 'col', axis=0)  22.6 us
    all_gather x1, waiting for transfers between devices, body(): partner = lax.all_gather(part, ('rx', 'core'), axis=0)  16.9 us
  transfers between devices with their start and end apart: 11, of which 7 were waited for; matrix products, arithmetic and copies ran while one was open for 9% of the time, Pallas kernels for 20%

profile of v3, /device:TPU:0, one launch (start us, length us, event | category | flops | bytes accessed | tf_op | source)
XLA Modules:
  0.0 374.6 jit_solution(3725615481883611051)
XLA Ops:
  6.5 0.9 select_reduce_fusion.1
  7.7 0.2 fusion
  7.8 0.2 select_reduce_fusion.2
  8.0 0.6 fusion.14
  8.6 0.6 fusion.13
  9.2 5.5 %pick.1 = f32[4,1024,256]{2,1,0:T(8,128)} custom-call(s32[4]{0:T(128)} %get-tuple-element.33.idx, s32[4]{0:T(128)} %get-tuple-element.31.loc, f32[1024,1024]{1,0:T(8,128)} %bitcast.130), custom_call_target="tpu_custom_call" | custom-call | tf_op jit(solution)/shard_map/pick/pallas_call | solution.py:33
  14.7 6.5 %all-to-all-start = ((f32[4,1024,256]{2,1,0:T(8,128)}), f32[4,1024,256]{2,1,0:T(8,128)}, u32[]{:S(2)}, u32[]{:S(2)}) async-start(f32[4,1024,256]{2,1,0:T(8,128)} %pick.1), calls=%async_computation | async-start | bytes 8388608 | tf_op jit(solution)/shard_map/all_to_all | solution.py:208
  21.2 0.6 dynamic_slice.62
  21.8 0.6 dynamic_slice.61
  23.7 2.0 dynamic-slice_select_fusion
  25.8 0.2 fusion.6
  25.9 0.6 gather_fusion.5
  26.6 0.6 gather_fusion.6
  27.2 0.1 select_reduce_fusion
  27.4 0.6 gather_fusion.2
  28.0 0.6 gather_fusion.4
  28.6 0.6 gather_fusion.3
  29.5 0.7 fusion.26
  30.1 1.3 compare_select_fusion.4
  31.6 0.6 gather_fusion.7
  32.3 0.6 stack.90.t
  32.9 16.9 %all-gather.6.cloned.1.call-done.partner.eb = bf16[4,256,1024]{2,1,0:T(8,128)(2,1)} async-done(((bf16[1,256,1024]{2,1,0:T(8,128)(2,1)}), bf16[4,256,1024]{2,1,0:T(8,128)(2,1)}) %all-gather.6.cloned.1.call-update) | async-done | bytes 2097168 | tf_op jit(solution)/shard_map/all_gather | solution.py:214
  49.8 5.6 %diag.1 = f32[512,512]{1,0:T(8,128)} custom-call(s32[8,4]{1,0:T(8,128)} %stack.90.t, f32[1024,1024]{1,0:T(8,128)} %bitcast.131, f32[768,1536]{1,0:T(8,128)} %front.5, bf16[1024,1024]{1,0:T(8,128)(2,1)} %bitcast.132, bf16[4,256,1024]{2,1,0:T(8,128)(2,1)} %all-gather.6.cloned.1.call-done.partner.eb), custom_call_target="tpu_custom_call" | custom-call | tf_op jit(solution)/shard_map/diag/pallas_call | solution.py:33
  56.1 0.2 fusion.7
  56.3 0.6 gather_fusion
  57.0 0.6 gather_fusion.1
  57.5 0.1 copy.24
  57.6 0.6 stack.91.t
  58.3 0.6 multiply_bitcast_fusion.fac
  58.9 55.7 %all-to-all-done.raw = f32[4,1024,256]{2,1,0:T(8,128)} async-done(((f32[4,1024,256]{2,1,0:T(8,128)}), f32[4,1024,256]{2,1,0:T(8,128)}, u32[]{:S(2)}, u32[]{:S(2)}) %all-to-all-start) | async-done | bytes 4194336 | tf_op jit(solution)/shard_map/all_to_all | solution.py:208
  114.6 15.4 %update.1.upd = f32[4,256,1024]{2,1,0:T(8,128)} custom-call(s32[4]{0:T(128)} %get-tuple-element.35.rows, s32[4,4]{1,0:T(4,128)} %multiply_bitcast_fusion.fac, f32[4,1024,256]{2,1,0:T(8,128)} %all-to-all-done.raw, bf16[1024,1024]{1,0:T(8,128)(2,1)} %bitcast.133, bf16[4,256,1024]{2,1,0:T(8,128)(2,1)} %all-gather.6.cloned.1.call-done.partner.eb), custom_call_target="tpu_custom_call" | custom-call | tf_op jit(solution)/shard_map/update/pallas_call | solution.py:33
  130.0 9.4 %strip.1 = f32[512,1536]{1,0:T(8,128)} custom-call(s32[5,12]{1,0:T(8,128)} %stack.91.t, f32[4,256,1024]{2,1,0:T(8,128)} %update.1.upd, f32[768,1536]{1,0:T(8,128)} %front.5), custom_call_target="tpu_custom_call" | custom-call | tf_op jit(solution)/shard_map/strip/pallas_call | solution.py:33
  139.5 0.5 all-reduce.2.cloned.1.call-update
  140.0 44.8 %reduce-scatter.5.cloned.1.call-done = f32[64,1536]{1,0:T(8,128)} async-done(((f32[512,1536]{1,0:T(8,128)}), f32[64,1536]{1,0:T(8,128)}) %reduce-scatter.5.cloned.1.call-update) | async-done | bytes 393232 | tf_op jit(solution)/shard_map/reduce_scatter | solution.py:276
  184.8 4.9 %all-to-all-start.1 = ((f32[4,256,1024]{2,1,0:T(8,128)}), f32[4,256,1024]{2,1,0:T(8,128)}, u32[]{:S(2)}, u32[]{:S(2)}) async-start(f32[4,256,1024]{2,1,0:T(8,128)} %update.1.upd), calls=%async_computation.1 | async-start | bytes 8388608 | tf_op jit(solution)/shard_map/all_to_all | solution.py:253
  189.8 31.9 %all-reduce.2.cloned.1.call-done = f32[64,512]{1,0:T(8,128)} async-done(((f32[64,512]{1,0:T(8,128)}), f32[64,512]{1,0:T(8,128)}) %all-reduce.2.cloned.1.call-update) | async-done | bytes 131088 | tf_op jit(solution)/shard_map/psum | solution.py:238
  222.2 0.2 all-gather.10.cloned.1.call-update
  223.5 1.2 stack.89.t
  224.7 12.5 %all-to-all-done.1.a0.a1 = f32[4,256,1024]{2,1,0:T(8,128)} async-done(((f32[4,256,1024]{2,1,0:T(8,128)}), f32[4,256,1024]{2,1,0:T(8,128)}, u32[]{:S(2)}, u32[]{:S(2)}) %all-to-all-start.1) | async-done | bytes 4194336 | tf_op jit(solution)/shard_map/all_to_all | solution.py:253
  237.2 22.6 %all-gather.12.cloned.1.call-done = f32[256,1536]{1,0:T(8,128)} async-done(((f32[64,1536]{1,0:T(8,128)}), f32[256,1536]{1,0:T(8,128)}) %all-gather.12.cloned.1.call-update) | async-done | bytes 1572880 | tf_op jit(solution)/shard_map/all_gather | solution.py:277
  259.8 1.5 fusion.25
  261.3 1.3 pad_maximum_fusion
  262.6 3.8 %all-to-all-start.2 = ((f32[8,64,768]{2,1,0:T(8,128)}), f32[8,64,768]{2,1,0:T(8,128)S(1)}, u32[]{:S(2)}, u32[]{:S(2)}) async-start(f32[8,64,768]{2,1,0:T(8,128)} %bitcast.27), calls=%async_computation.4 | async-start | bytes 3145728 | tf_op jit(solution)/shard_map/all_to_all | solution.py:281
  266.4 22.9 %all-gather.8.cloned.1.call-done.a_in = f32[512,512]{1,0:T(8,128)} async-done(((f32[64,512]{1,0:T(8,128)}), f32[512,512]{1,0:T(8,128)}) %all-gather.8.cloned.1.call-update) | async-done | bytes 1048592 | tf_op jit(solution)/shard_map/all_gather | solution.py:238
  289.3 46.0 %factor.1 = f32[512,512]{1,0:T(8,128)} custom-call(f32[512,512]{1,0:T(8,128)} %all-gather.8.cloned.1.call-done.a_in), custom_call_target="tpu_custom_call" | custom-call | flops 40000000000 | bytes 2097152 | tf_op jit(solution)/shard_map/factor/pallas_call | solution.py:149
  335.3 5.2 %fusion.27.wr = f32[512,768]{1,0:T(8,128)} fusion(f32[512,512]{1,0:T(8,128)} %factor.1, f32[512,768]{1,0:T(8,128)S(1)} %bitcast.134), kind=kOutput, calls=%fused_computation.149 | convolution fusion | flops 2415919104 | bytes 4194304 | tf_op jit(solution)/shard_map/dot_general | solution.py:284
  340.5 8.1 %fusion.28.wc = f32[512,1536]{1,0:T(8,128)} fusion(f32[512,512]{1,0:T(8,128)S(1)} %copy-done.1, f32[512,1536]{1,0:T(8,128)} %all-gather.10.cloned.1.call-done), kind=kOutput, calls=%fused_computation.150 | convolution fusion | flops 4831838208 | bytes 7340032 | tf_op jit(solution)/shard_map/dot_general | solution.py:283
  348.6 19.1 %final.1 = f32[768,1536]{1,0:T(8,128)} custom-call(s32[13,18]{1,0:T(8,128)} %stack.89.t, f32[768,1536]{1,0:T(8,128)} %front.5, f32[4,256,1024]{2,1,0:T(8,128)} %all-to-all-done.1.a0.a1, f32[4,256,1024]{2,1,0:T(8,128)} %collective-permute-done.b0.b1, f32[4,256,1024]{2,1,0:T(8,128)} %all-to-all-done.1.a0.a1, f32[4,256,1024]{2,1,0:T(8,128)} %collective-permute-done.b0.b1, ...), custom_call_target="tpu_custom_call" | custom-call | tf_op jit(solution)/shard_map/final/pallas_call | solution.py:33
  (92 shorter events, 3.4 us)
Async XLA Ops:
  6.5 25.1 %copy-start = (s32[2,16,16]{2,1,0:T(8,128)S(1)}, s32[2,16,16]{2,1,0:T(8,128)}, u32[]{:S(2)}) copy-start(s32[2,16,16]{2,1,0:T(8,128)} %param.10) | copy-start | bytes 6148
  14.7 11.0 %copy-start.2 = (s32[24]{0:T(128)S(1)}, s32[24]{0:T(128)}, u32[]{:S(2)}) copy-start(s32[24]{0:T(128)} %param.12) | copy-start | bytes 292
  14.7 11.0 %copy-start.4 = (s32[4]{0:T(128)S(1)}, s32[4]{0:T(128)}, u32[]{:S(2)}) copy-start(s32[4]{0:T(128)} %constant.304) | copy-start | bytes 52
  14.7 11.9 %copy-start.3 = (s32[4]{0:T(128)S(1)}, s32[4]{0:T(128)}, u32[]{:S(2)}) copy-start(s32[4]{0:T(128)} %constant.305) | copy-start | bytes 52
  14.7 99.9 %all-to-all-start = ((f32[4,1024,256]{2,1,0:T(8,128)}), f32[4,1024,256]{2,1,0:T(8,128)}, u32[]{:S(2)}, u32[]{:S(2)}) async-start(f32[4,1024,256]{2,1,0:T(8,128)} %pick.1), calls=%async_computation | async-start | bytes 8388608 | tf_op jit(solution)/shard_map/all_to_all | solution.py:208
  21.2 28.6 %all-gather.6.cloned.1.call-start = ((), (), s32[]{:S(2)}) async-start(), calls=%async_computation.5 | async-start | bytes 2621440 | tf_op jit(solution)/shard_map/all_gather | solution.py:214
  25.6 113.8 %reduce-scatter.3.cloned.1.call-start = ((), (), s32[]{:S(2)}) async-start(), calls=%async_computation.6 | async-start | bytes 1179648 | tf_op jit(solution)/shard_map/reduce_scatter | solution.py:237
  55.4 129.4 %reduce-scatter.5.cloned.1.call-start = ((), (), s32[]{:S(2)}) async-start(), calls=%async_computation.9 | async-start | bytes 3538944 | tf_op jit(solution)/shard_map/reduce_scatter | solution.py:276
  139.4 82.3 %all-reduce.2.cloned.1.call-start = ((), (), s32[]{:S(2)}) async-start(), calls=%async_computation.7 | async-start | bytes 262144 | tf_op jit(solution)/shard_map/psum | solution.py:238
  140.0 119.9 %all-gather.12.cloned.1.call-start = ((), (), s32[]{:S(2)}) async-start(), calls=%async_computation.11 | async-start | bytes 1966080 | tf_op jit(solution)/shard_map/all_gather | solution.py:277
  184.8 52.4 %all-to-all-start.1 = ((f32[4,256,1024]{2,1,0:T(8,128)}), f32[4,256,1024]{2,1,0:T(8,128)}, u32[]{:S(2)}, u32[]{:S(2)}) async-start(f32[4,256,1024]{2,1,0:T(8,128)} %update.1.upd), calls=%async_computation.1 | async-start | bytes 8388608 | tf_op jit(solution)/shard_map/all_to_all | solution.py:253
  189.7 99.6 %all-gather.8.cloned.1.call-start = ((), (), s32[]{:S(2)}) async-start(), calls=%async_computation.8 | async-start | bytes 1179648 | tf_op jit(solution)/shard_map/all_gather | solution.py:238
  221.7 118.9 %all-gather.10.cloned.1.call-start = ((), (), s32[]{:S(2)}) async-start(), calls=%async_computation.10 | async-start | bytes 3538944 | tf_op jit(solution)/shard_map/all_gather | solution.py:278
  237.2 111.4 %collective-permute-start = (f32[4,256,1024]{2,1,0:T(8,128)}, f32[4,256,1024]{2,1,0:T(8,128)}, u32[]{:S(2)}, u32[]{:S(2)}) collective-permute-start(f32[4,256,1024]{2,1,0:T(8,128)} %all-to-all-done.1.a0.a1), channel_id=1, source_target_pairs={{0,4},{4,0},{1,5},{5,1},{2,6},{6,2},{3,7},{7,3},{8,12},{12,8},{9,1... | collective-permute-start | bytes 12582920 | tf_op jit(solution)/shard_map/ppermute | solution.py:254
  262.6 72.7 %all-to-all-start.2 = ((f32[8,64,768]{2,1,0:T(8,128)}), f32[8,64,768]{2,1,0:T(8,128)S(1)}, u32[]{:S(2)}, u32[]{:S(2)}) async-start(f32[8,64,768]{2,1,0:T(8,128)} %bitcast.27), calls=%async_computation.4 | async-start | bytes 3145728 | tf_op jit(solution)/shard_map/all_to_all | solution.py:281
  335.3 5.2 %copy-start.1 = (f32[512,512]{1,0:T(8,128)S(1)}, f32[512,512]{1,0:T(8,128)}, u32[]{:S(2)}) copy-start(f32[512,512]{1,0:T(8,128)} %factor.1) | copy-start | bytes 3145732
Sparse Core Ops, SparseCore 0:
  25.8 24.0 all-gather.5
  55.5 35.7 reduce-scatter.2
  139.5 45.2 reduce-scatter.4
  187.0 34.6 all-reduce.1
  223.1 36.7 all-gather.11
  261.6 27.6 all-gather.7
  291.2 32.3 all-gather.9

commit v4 on v3

--- a/solution.py
+++ b/solution.py
@@ -10,6 +10,9 @@
 TILE = 256
 F32 = jnp.float32
 BF16 = jnp.bfloat16
+META = 16
+CODED = TILE + META
+FULL = 32767.0
 NT = (((1,), (1,)), ((), ()))
 TN = (((0,), (0,)), ((), ()))
 
@@ -42,9 +45,34 @@
     )(*tables, *operands)
 
 
-def pick_kernel(idx, loc, src, out):
-    ok = loc[pl.program_id(0)] != 0
-    out[0] = jnp.where(ok, src[...], jnp.zeros_like(src))
+def powers(k):
+    h = jnp.floor(k * 0.5)
+    return jnp.exp2(h), jnp.exp2(k - h)
+
+
+def encode(x):
+    top = jnp.maximum(jnp.max(jnp.abs(x), axis=0, keepdims=True), 1e-37)
+    k = jnp.ceil(jnp.log2(top) + 1e-3)
+    p, r = powers(-k)
+    part = jnp.clip(jnp.ceil(top * p * r * FULL), 1.0, FULL)
+    q = jnp.clip(x * p * (r * (FULL * FULL / part)), -FULL, FULL)
+    q = jnp.floor(q + 0.5).astype(jnp.int32)
+    ids = lax.broadcasted_iota(jnp.int32, (META, TILE), 0)
+    meta = jnp.where(ids == 0, k.astype(jnp.int32), jnp.where(ids == 1, part.astype(jnp.int32), 0))
+    return q.astype(jnp.int16), meta.astype(jnp.int16)
+
+
+def decode(code):
+    meta = code[TILE:, :].astype(jnp.int32).astype(F32)
+    p, r = powers(meta[0:1, :])
+    q = code[:TILE, :].astype(jnp.int32).astype(F32)
+    return q * (meta[1:2, :] * (1.0 / (FULL * FULL)) * p) * r
+
+
+def pick_kernel(idx, src, out):
+    q, meta = encode(src[...])
+    out[0, 0, :TILE, :] = q
+    out[0, 0, TILE:, :] = meta
 
 
 def diag_kernel(t, blk, front, ea, eb, out):
@@ -53,10 +81,14 @@
     out[...] = x - jnp.where(t[6, k] != 0, dot(ea[...], eb[0], NT), 0.0)
 
 
-def update_kernel(rows, fac, raw, panel, partner, out):
+def update_kernel(rows, fac, raw, panel, partner, out, coded):
     f = fac[pl.program_id(0), pl.program_id(1)]
-    u = raw[0] - dot(panel[...], partner[0], NT)
-    out[0] = jnp.where(f != 0, u, 0.0)
+    u = decode(raw[0, 0]) - dot(panel[...], partner[0], NT)
+    u = jnp.where(f != 0, u, 0.0)
+    out[0] = u
+    q, meta = encode(u)
+    coded[0, :TILE, :] = q
+    coded[0, TILE:, :] = meta
 
 
 def strip_kernel(t, upd, front, out):
@@ -71,10 +103,12 @@
 
     @pl.when(panel == 0)
     def _():
-        x = front[...]
+        out[...] = front[...] - dot3(wr[...], wc[...], TN)
         for m, src in enumerate((a0, b0, a1, b1)):
-            x = x + jnp.where(t[8 + m, k] != 0, src[0], 0.0)
-        out[...] = x - dot3(wr[...], wc[...], TN)
+
+            @pl.when(t[8 + m, k] != 0)
+            def _(src=src):
+                out[...] = out[...] + decode(src[0])
 
     @pl.when(panel == 1)
     def _():
@@ -193,17 +227,16 @@
     row_tile = lax.dynamic_index_in_dim(which, row, 0, keepdims=False)
     row_ok = lax.dynamic_index_in_dim(there, row, 0, keepdims=False)
     out_tile = lax.dynamic_index_in_dim(which, col, 0, keepdims=False)
-    out_ok = lax.dynamic_index_in_dim(there, col, 0, keepdims=False)
     in_tile = lax.dynamic_index_in_dim(which, col, 1, keepdims=False)
     in_ok = lax.dynamic_index_in_dim(there, col, 1, keepdims=False)
     e = parent_place[:2]
     ie = inv_own[e]
 
     outgoing = tile_call(
-        pick_kernel, (blocks,), (out_tile, out_ok), (block,),
-        [pl.BlockSpec((width, TILE), lambda z, i, l: (0, i[z]))],
-        jax.ShapeDtypeStruct((blocks, width, TILE), F32),
-        pl.BlockSpec((1, width, TILE), lambda z, i, l: (z, 0, 0)), "pick",
+        pick_kernel, (blocks, td), (out_tile,), (block,),
+        [pl.BlockSpec((TILE, TILE), lambda z, r, i: (r, i[z]))],
+        jax.ShapeDtypeStruct((blocks, td, CODED, TILE), jnp.int16),
+        pl.BlockSpec((1, 1, CODED, TILE), lambda z, r, i: (z, r, 0, 0)), "pick",
     )
     raw = lax.all_to_all(outgoing, "col", split_axis=0, concat_axis=0, tiled=True)
 
@@ -234,23 +267,33 @@
         pl.BlockSpec((TILE, TILE), lambda a, b, t: (a, b)), "diag",
     )
     plane = ("child", "rx", "core")
-    diagonal = lax.psum_scatter(diag_part, plane, scatter_dimension=0, tiled=True)
-    diagonal = lax.all_gather(lax.psum(diagonal, "col"), plane, axis=0, tiled=True)
+    every = ("child", "rx", "core", "col")
+    devices = lax.axis_size(every)
+    diagonal = diag_part.reshape(devices, 2 * TILE // devices, 2 * TILE)
+    diagonal = lax.all_to_all(diagonal, every, split_axis=0, concat_axis=0, tiled=True)
+    diagonal, partner = lax.optimization_barrier((jnp.sum(diagonal, axis=0), partner))
+    diagonal = lax.all_gather(diagonal, every, axis=0, tiled=True)
     inverse = factor_inverse(diagonal)
 
     col_ids = jnp.arange(blocks, dtype=i32) * td + in_tile
     factors = pat[row * td + row_tile][:, col_ids] * row_ok[:, None] * in_ok[None, :]
-    update = tile_call(
+    update, coded = tile_call(
         update_kernel, (chips, blocks), (row_tile, factors), (raw, own, partner),
         [
-            pl.BlockSpec((1, TILE, TILE), lambda p, b, r, f: (b, r[p], 0)),
+            pl.BlockSpec((1, 1, CODED, TILE), lambda p, b, r, f: (b, r[p], 0, 0)),
             pl.BlockSpec((TILE, depth), lambda p, b, r, f: (r[p], 0)),
             pl.BlockSpec((1, TILE, depth), lambda p, b, r, f: (b, 0, 0)),
         ],
-        jax.ShapeDtypeStruct((chips, TILE, blocks * TILE), F32),
-        pl.BlockSpec((1, TILE, TILE), lambda p, b, r, f: (p, 0, b)), "update",
-    )
-    first = lax.all_to_all(update, ("child", "rx"), split_axis=0, concat_axis=0, tiled=True)
+        [
+            jax.ShapeDtypeStruct((chips, TILE, blocks * TILE), F32),
+            jax.ShapeDtypeStruct((chips, CODED, blocks * TILE), jnp.int16),
+        ],
+        [
+            pl.BlockSpec((1, TILE, TILE), lambda p, b, r, f: (p, 0, b)),
+            pl.BlockSpec((1, CODED, TILE), lambda p, b, r, f: (p, 0, b)),
+        ], "update",
+    )
+    first = lax.all_to_all(coded, ("child", "rx"), split_axis=0, concat_axis=0, tiled=True)
     second = lax.ppermute(first, "core", [(k, (k + 1) % 2) for k in range(2)])
 
     my_cols = lax.dynamic_slice_in_dim(inv, col * cd, cd, 1)
@@ -303,7 +346,7 @@
 
     def from_list(n):
         return pl.BlockSpec(
-            (1, TILE, TILE), lambda i, j, t: (t[n, i * cd + j], 0, t[4 + n, i * cd + j])
+            (1, CODED, TILE), lambda i, j, t: (t[n, i * cd + j], 0, t[4 + n, i * cd + j])
         )
 
     return tile_call(

time: 377 us -> 382 us (1.013)
  Pallas kernels: 101 us -> 107 us
  waiting for transfers between devices: 208 us -> 203 us
    psum x1 -> x0, waiting for transfers between devices: 31.9 us -> none  [body(): lax.psum(diagonal, 'col')]
    all_gather x1, waiting for transfers between devices: 22.9 us -> 48.3 us  [body(): diagonal = lax.all_gather(diagonal, every, axis=0, tiled=True)]
    all_to_all x1 -> x2, waiting for transfers between devices: 12.5 us -> 36.7 us  [the longest x1 23.4 us: body(): lax.all_to_all(coded, ('child', 'rx'), split_axis=0, concat_axis=0, tiled...]
    all_gather x1, waiting for transfers between devices: 22.6 us -> 7.8 us  [body(): pieces = lax.all_gather(piece, 'col', axis=0)]
    all_to_all x1, waiting for transfers between devices: 55.7 us -> 45.7 us  [body(): lax.all_to_all(outgoing, 'col', split_axis=0, concat_axis=0, tiled=True)]
    pallas_call x5, Pallas kernels: 55 us -> 60.6 us  [tile_call(): pl.pallas_call(kernel, grid_spec=pltpu.PrefetchScalarGridSpec(num_scalar_...]
    all_to_all x1 -> x2, starting transfers between devices: 4.87 us -> 8.23 us  [the longest x1 4.6 us: body(): lax.all_to_all(diagonal, every, split_axis=0, concat_axis=0, tiled=True)]
  transfers between devices with their start and end apart: 11 -> 10, of which waited for: 7 -> 7; matrix products, arithmetic and copies ran while one was open for 9% -> 9% of each run, Pallas kernels for 20% -> 15%
where the time goes in v4:
time: 382 us; the launch traced here: 380 us
  waiting for transfers between devices  203 us (53%)
  Pallas kernels  107 us (28%)
  starting transfers between devices  17.4 us (5%)
  between operations  14.6 us (4%)
  local copies, waits for them, and re-layouts  14.3 us (4%)
  matrix products  13.8 us (4%)
  other arithmetic  10.7 us (3%)
    pallas_call x5, Pallas kernels, tile_call(): pl.pallas_call(kernel, grid_spec=pltpu.PrefetchScalarGridSpec(num_scalar_...  60.6 us
    all_gather x1, waiting for transfers between devices, body(): diagonal = lax.all_gather(diagonal, every, axis=0, tiled=True)  48.3 us
    pallas_call x1, Pallas kernels, factor_inverse(): pl.pallas_call(factor_kernel, out_shape=jax.ShapeDtypeStruct(d.shape, F32...  46 us
    all_to_all x1, waiting for transfers between devices, body(): lax.all_to_all(outgoing, 'col', split_axis=0, concat_axis=0, tiled=True)  45.7 us
    reduce_scatter x1, waiting for transfers between devices, body(): piece = lax.psum_scatter(strip_part, plane, scatter_dimension=0, tiled=True)  44.4 us
    all_to_all x1, waiting for transfers between devices, body(): lax.all_to_all(coded, ('child', 'rx'), split_axis=0, concat_axis=0, tiled...  23.4 us
    all_gather x1, waiting for transfers between devices, body(): partner = lax.all_gather(part, ('rx', 'core'), axis=0)  18.8 us
    all_to_all x1, waiting for transfers between devices, body(): lax.all_to_all(diagonal, every, split_axis=0, concat_axis=0, tiled=True)  13.3 us
  transfers between devices with their start and end apart: 10, of which 7 were waited for; matrix products, arithmetic and copies ran while one was open for 9% of the time, Pallas kernels for 15%

profile of v4, /device:TPU:0, one launch (start us, length us, event | category | flops | bytes accessed | tf_op | source)
XLA Modules:
  0.0 380.0 jit_solution(13898723234163611045)
XLA Ops:
  6.5 0.9 select_reduce_fusion.1
  8.0 0.6 dynamic_slice.59
  9.2 0.6 dynamic_slice.58
  10.5 1.9 dynamic-slice_select_fusion
  12.5 0.7 pad_clamp_fusion.1
  13.1 0.7 broadcast_add_fusion.5
  13.8 0.6 gather_fusion.5
  14.4 0.7 pad_clamp_fusion
  15.1 0.6 gather_fusion.6
  15.9 0.6 gather_fusion.2
  16.5 0.6 gather_fusion.4
  17.1 0.6 gather_fusion.3
  17.8 0.6 gather_fusion.7
  18.5 0.6 stack.90.t
  19.1 18.8 %all-gather.6.cloned.1.call-done.eb.partner = bf16[4,256,1024]{2,1,0:T(8,128)(2,1)} async-done(((bf16[1,256,1024]{2,1,0:T(8,128)(2,1)}), bf16[4,256,1024]{2,1,0:T(8,128)(2,1)}) %all-gather.6.cloned.1.call-update) | async-done | bytes 2097168 | tf_op jit(solution)/shard_map/all_gather | solution.py:247
  37.9 5.6 %diag.1 = f32[512,512]{1,0:T(8,128)} custom-call(s32[8,4]{1,0:T(8,128)} %stack.90.t, f32[1024,1024]{1,0:T(8,128)} %bitcast.129, f32[768,1536]{1,0:T(8,128)} %front.5, bf16[1024,1024]{1,0:T(8,128)(2,1)} %bitcast.131, bf16[4,256,1024]{2,1,0:T(8,128)(2,1)} %all-gather.6.cloned.1.call-done.eb.partner), custom_call_target="tpu_custom_call" | custom-call | tf_op jit(solution)/shard_map/diag/pallas_call | solution.py:36
  43.5 4.6 %all-to-all-start.1 = ((f32[32,16,512]{2,1,0:T(8,128)}), f32[32,16,512]{2,1,0:T(8,128)S(1)}, u32[]{:S(2)}, u32[]{:S(2)}) async-start(f32[32,16,512]{2,1,0:T(8,128)} %bitcast.134), calls=%async_computation.1 | async-start | bytes 2097152 | tf_op jit(solution)/shard_map/all_to_all | solution.py:273
  48.1 0.5 fusion.13
  48.6 11.1 %pick.1 = s16[4,4,272,256]{3,2,1,0:T(8,128)(2,1)} custom-call(s32[4]{0:T(128)} %get-tuple-element.39.idx, f32[1024,1024]{1,0:T(8,128)} %bitcast.130), custom_call_target="tpu_custom_call" | custom-call | tf_op jit(solution)/shard_map/pick/pallas_call | solution.py:36
  59.7 13.3 %all-to-all-done.1 = f32[32,16,512]{2,1,0:T(8,128)S(1)} async-done(((f32[32,16,512]{2,1,0:T(8,128)}), f32[32,16,512]{2,1,0:T(8,128)S(1)}, u32[]{:S(2)}, u32[]{:S(2)}) %all-to-all-start.1) | async-done | bytes 1048608 | tf_op jit(solution)/shard_map/all_to_all | solution.py:273
  73.0 4.6 %all-to-all-start = ((s16[4,4,272,256]{3,2,1,0:T(8,128)(2,1)}), s16[4,4,272,256]{3,2,1,0:T(8,128)(2,1)S(1)}, u32[]{:S(2)}, u32[]{:S(2)}) async-start(s16[4,4,272,256]{3,2,1,0:T(8,128)(2,1)} %pick.1), calls=%async_computation | async-start | bytes 4456448 | tf_op jit(solution)/shard_map/all_to_all | solution.py:241
  77.9 0.6 fusion.25
  78.5 1.2 compare_select_fusion.4
  80.5 0.2 fusion.7
  80.7 0.6 gather_fusion
  81.4 0.6 gather_fusion.1
  82.0 0.6 stack.91.t
  82.7 0.7 multiply_bitcast_fusion.fac
  83.3 0.7 reduce_sum.39
  84.0 45.7 %all-to-all-done.raw = s16[4,4,272,256]{3,2,1,0:T(8,128)(2,1)S(1)} async-done(((s16[4,4,272,256]{3,2,1,0:T(8,128)(2,1)}), s16[4,4,272,256]{3,2,1,0:T(8,128)(2,1)S(1)}, u32[]{:S(2)}, u32[]{:S(2)}) %all-to-all-start) | async-done | bytes 2228256 | tf_op jit(solution)/shard_map/all_to_all | solution.py:241
  129.7 1.4 copy-done.2
  131.1 15.5 %update.1 = (f32[4,256,1024]{2,1,0:T(8,128)}, s16[4,272,1024]{2,1,0:T(8,128)(2,1)}) custom-call(s32[4]{0:T(128)} %get-tuple-element.41.rows, s32[4,4]{1,0:T(4,128)} %multiply_bitcast_fusion.fac, s16[4,4,272,256]{3,2,1,0:T(8,128)(2,1)} %copy-done.2, bf16[1024,1024]{1,0:T(8,128)(2,1)} %bitcast.132, bf16[4,256,1024]{2,1,0:T(8,128)(2,1)} %all-gather.6.cloned.1.call-done.eb.partner), custom_call_target="tpu_custom_call" | custom-call | tf_op jit(solution)/shard_map/update/pallas_call | solution.py:36
  146.6 9.4 %strip.1 = f32[512,1536]{1,0:T(8,128)} custom-call(s32[5,12]{1,0:T(8,128)} %stack.91.t, f32[4,256,1024]{2,1,0:T(8,128)} %get-tuple-element.12.upd, f32[768,1536]{1,0:T(8,128)} %front.5), custom_call_target="tpu_custom_call" | custom-call | tf_op jit(solution)/shard_map/strip/pallas_call | solution.py:36
  156.0 44.4 %reduce-scatter.2.cloned.1.call-done = f32[64,1536]{1,0:T(8,128)} async-done(((f32[512,1536]{1,0:T(8,128)}), f32[64,1536]{1,0:T(8,128)}) %reduce-scatter.2.cloned.1.call-update) | async-done | bytes 393232 | tf_op jit(solution)/shard_map/reduce_scatter | solution.py:319
  200.5 0.5 all-gather.8.cloned.1.call-update
  201.3 3.6 all-to-all-start.2
  205.3 0.3 all-gather.10.cloned.1.call-update
  206.7 1.2 stack.89.t
  207.9 23.4 %all-to-all-done.2.a0.a1 = s16[4,272,1024]{2,1,0:T(8,128)(2,1)S(1)} async-done(((s16[4,272,1024]{2,1,0:T(8,128)(2,1)}), s16[4,272,1024]{2,1,0:T(8,128)(2,1)S(1)}, u32[]{:S(2)}, u32[]{:S(2)}) %all-to-all-start.2) | async-done | bytes 2228256 | tf_op jit(solution)/shard_map/all_to_all | solution.py:296
  231.3 7.8 %all-gather.12.cloned.1.call-done = f32[256,1536]{1,0:T(8,128)} async-done(((f32[64,1536]{1,0:T(8,128)}), f32[256,1536]{1,0:T(8,128)}) %all-gather.12.cloned.1.call-update) | async-done | bytes 1572880 | tf_op jit(solution)/shard_map/all_gather | solution.py:320
  239.1 1.5 fusion.24
  240.6 1.3 pad_maximum_fusion
  241.9 4.5 %all-to-all-start.3 = ((f32[8,64,768]{2,1,0:T(8,128)}), f32[8,64,768]{2,1,0:T(8,128)}, u32[]{:S(2)}, u32[]{:S(2)}) async-start(f32[8,64,768]{2,1,0:T(8,128)} %bitcast.133), calls=%async_computation.4 | async-start | bytes 3145728 | tf_op jit(solution)/shard_map/all_to_all | solution.py:324
  246.3 48.3 %all-gather.8.cloned.1.call-done.a_in = f32[512,512]{1,0:T(8,128)} async-done(((f32[16,512]{1,0:T(8,128)}), f32[512,512]{1,0:T(8,128)}) %all-gather.8.cloned.1.call-update) | async-done | bytes 1048592 | tf_op jit(solution)/shard_map/all_gather | solution.py:275
  294.7 46.0 %factor.1 = f32[512,512]{1,0:T(8,128)} custom-call(f32[512,512]{1,0:T(8,128)} %all-gather.8.cloned.1.call-done.a_in), custom_call_target="tpu_custom_call" | custom-call | flops 40000000000 | bytes 2097152 | tf_op jit(solution)/shard_map/factor/pallas_call | solution.py:183
  340.7 5.8 %fusion.26.wr = f32[512,768]{1,0:T(8,128)} fusion(f32[512,512]{1,0:T(8,128)} %factor.1, f32[512,768]{1,0:T(8,128)} %bitcast.28), kind=kOutput, calls=%fused_computation.147 | convolution fusion | flops 2415919104 | bytes 4194304 | tf_op jit(solution)/shard_map/dot_general | solution.py:327
  346.4 8.0 %fusion.27.wc = f32[512,1536]{1,0:T(8,128)} fusion(f32[512,512]{1,0:T(8,128)S(1)} %copy-done.3, f32[512,1536]{1,0:T(8,128)} %all-gather.10.cloned.1.call-done), kind=kOutput, calls=%fused_computation.148 | convolution fusion | flops 4831838208 | bytes 7340032 | tf_op jit(solution)/shard_map/dot_general | solution.py:326
  354.5 19.0 %final.1 = f32[768,1536]{1,0:T(8,128)} custom-call(s32[13,18]{1,0:T(8,128)} %stack.89.t, f32[768,1536]{1,0:T(8,128)} %front.5, s16[4,272,1024]{2,1,0:T(8,128)(2,1)} %copy-done.1, s16[4,272,1024]{2,1,0:T(8,128)(2,1)} %collective-permute-done.b0.b1, s16[4,272,1024]{2,1,0:T(8,128)(2,1)} %copy-done.1, s16[4,272,1024]{2,1,0:T(8,128)(2,1)} %collective-permute-done.b0.b1, ...), custom_call_target="tpu_custom_call" | custom-call | tf_op jit(solution)/shard_map/final/pallas_call | solution.py:36
  (89 shorter events, 3.9 us)
Async XLA Ops:
  6.5 11.2 %copy-start = (s32[2,16,16]{2,1,0:T(8,128)S(1)}, s32[2,16,16]{2,1,0:T(8,128)}, u32[]{:S(2)}) copy-start(s32[2,16,16]{2,1,0:T(8,128)} %param.10) | copy-start | bytes 6148
  6.5 31.4 %all-gather.6.cloned.1.call-start = ((), (), s32[]{:S(2)}) async-start(), calls=%async_computation.5 | async-start | bytes 2621440 | tf_op jit(solution)/shard_map/all_gather | solution.py:247
  43.5 29.5 %all-to-all-start.1 = ((f32[32,16,512]{2,1,0:T(8,128)}), f32[32,16,512]{2,1,0:T(8,128)S(1)}, u32[]{:S(2)}, u32[]{:S(2)}) async-start(f32[32,16,512]{2,1,0:T(8,128)} %bitcast.134), calls=%async_computation.1 | async-start | bytes 2097152 | tf_op jit(solution)/shard_map/all_to_all | solution.py:273
  59.7 18.2 %copy-start.4 = (s32[24]{0:T(128)S(1)}, s32[24]{0:T(128)}, u32[]{:S(2)}) copy-start(s32[24]{0:T(128)} %param.12) | copy-start | bytes 292
  73.0 56.7 %all-to-all-start = ((s16[4,4,272,256]{3,2,1,0:T(8,128)(2,1)}), s16[4,4,272,256]{3,2,1,0:T(8,128)(2,1)S(1)}, u32[]{:S(2)}, u32[]{:S(2)}) async-start(s16[4,4,272,256]{3,2,1,0:T(8,128)(2,1)} %pick.1), calls=%async_computation | async-start | bytes 4456448 | tf_op jit(solution)/shard_map/all_to_all | solution.py:241
  77.6 122.9 %reduce-scatter.2.cloned.1.call-start = ((), (), s32[]{:S(2)}) async-start(), calls=%async_computation.7 | async-start | bytes 3538944 | tf_op jit(solution)/shard_map/reduce_scatter | solution.py:319
  129.7 1.4 copy-start.2
  156.0 83.1 %all-gather.12.cloned.1.call-start = ((), (), s32[]{:S(2)}) async-start(), calls=%async_computation.9 | async-start | bytes 1966080 | tf_op jit(solution)/shard_map/all_gather | solution.py:320
  200.5 94.2 %all-gather.8.cloned.1.call-start = ((), (), s32[]{:S(2)}) async-start(), calls=%async_computation.6 | async-start | bytes 1081344 | tf_op jit(solution)/shard_map/all_gather | solution.py:275
  201.3 30.0 %all-to-all-start.2 = ((s16[4,272,1024]{2,1,0:T(8,128)(2,1)}), s16[4,272,1024]{2,1,0:T(8,128)(2,1)S(1)}, u32[]{:S(2)}, u32[]{:S(2)}) async-start(s16[4,272,1024]{2,1,0:T(8,128)(2,1)} %get-tuple-element.10), calls=%async_computation.2 | async-start | bytes 4456448 | tf_op jit(solution)/shard_map/all_to_all | solution.py:296
  204.9 141.5 %all-gather.10.cloned.1.call-start = ((), (), s32[]{:S(2)}) async-start(), calls=%async_computation.8 | async-start | bytes 3538944 | tf_op jit(solution)/shard_map/all_gather | solution.py:321
  231.3 10.6 %copy-start.1 = (s16[4,272,1024]{2,1,0:T(8,128)(2,1)}, s16[4,272,1024]{2,1,0:T(8,128)(2,1)S(1)}, u32[]{:S(2)}) copy-start(s16[4,272,1024]{2,1,0:T(8,128)(2,1)S(1)} %all-to-all-done.2.a0.a1) | copy-start | bytes 6684676
  231.3 123.2 %collective-permute-start = (s16[4,272,1024]{2,1,0:T(8,128)(2,1)S(1)}, s16[4,272,1024]{2,1,0:T(8,128)(2,1)}, u32[]{:S(2)}, u32[]{:S(2)}) collective-permute-start(s16[4,272,1024]{2,1,0:T(8,128)(2,1)S(1)} %all-to-all-done.2.a0.a1), channel_id=1, source_target_pairs={{0,4},{4,0},{1,5},{5,1},{2,6},{6,2},{3,7},{7,3},{8,12},{12,8},{9,1... | collective-permute-start | bytes 6684680 | tf_op jit(solution)/shard_map/ppermute | solution.py:297
  241.9 98.8 %all-to-all-start.3 = ((f32[8,64,768]{2,1,0:T(8,128)}), f32[8,64,768]{2,1,0:T(8,128)}, u32[]{:S(2)}, u32[]{:S(2)}) async-start(f32[8,64,768]{2,1,0:T(8,128)} %bitcast.133), calls=%async_computation.4 | async-start | bytes 3145728 | tf_op jit(solution)/shard_map/all_to_all | solution.py:324
  340.7 5.8 %copy-start.3 = (f32[512,512]{1,0:T(8,128)S(1)}, f32[512,512]{1,0:T(8,128)}, u32[]{:S(2)}) copy-start(f32[512,512]{1,0:T(8,128)} %factor.1) | copy-start | bytes 3145732
Sparse Core Ops, SparseCore 0:
  12.6 25.2 all-gather.5
  156.1 44.2 reduce-scatter.1
  202.0 37.0 all-gather.11
  241.9 52.6 all-gather.7
  296.4 31.2 all-gather.9

commit v5 on v4

--- a/solution.py
+++ b/solution.py
@@ -14,7 +14,7 @@
 CODED = TILE + META
 FULL = 32767.0
 NT = (((1,), (1,)), ((), ()))
-TN = (((0,), (0,)), ((), ()))
+NN = (((1,), (0,)), ((), ()))
 
 
 def dot(a, b, dims):
@@ -24,12 +24,6 @@
 def split(x):
     hi = x.astype(BF16)
     return hi, (x - hi.astype(F32)).astype(BF16)
-
-
-def dot3(a, b, dims):
-    ah, al = split(a)
-    bh, bl = split(b)
-    return dot(ah, bh, dims) + (dot(ah, bl, dims) + dot(al, bh, dims))
 
 
 def tile_call(kernel, grid, tables, operands, in_specs, out_shape, out_spec, name, cost=None, scratch=()):
@@ -97,13 +91,19 @@
     out[...] = jnp.where(t[2, k] != 0, upd[0], 0.0) + jnp.where(t[4, k] != 0, front[...], 0.0)
 
 
-def final_kernel(t, front, a0, b0, a1, b1, wr, wc, out):
+def final_kernel(t, front, a0, b0, a1, b1, wr, wc, out, wrh, wrl):
     k = pl.program_id(0) * pl.num_programs(1) + pl.program_id(1)
     panel = t[12, k]
 
+    @pl.when(pl.program_id(1) == 0)
+    def _():
+        wrh[...], wrl[...] = split(wr[...])
+
     @pl.when(panel == 0)
     def _():
-        out[...] = front[...] - dot3(wr[...], wc[...], TN)
+        wch, wcl = split(wc[...])
+        big = dot(wrh[...], wch, NN)
+        out[...] = front[...] - (big + (dot(wrh[...], wcl, NN) + dot(wrl[...], wch, NN)))
         for m, src in enumerate((a0, b0, a1, b1)):
 
             @pl.when(t[8 + m, k] != 0)
@@ -112,11 +112,11 @@
 
     @pl.when(panel == 1)
     def _():
-        out[...] = wr[:TILE, :].T
+        out[...] = wr[:, :TILE]
 
     @pl.when(panel == 2)
     def _():
-        out[...] = wr[TILE:, :].T
+        out[...] = wr[:, TILE:]
 
 
 BASE = 128
@@ -271,8 +271,8 @@
     devices = lax.axis_size(every)
     diagonal = diag_part.reshape(devices, 2 * TILE // devices, 2 * TILE)
     diagonal = lax.all_to_all(diagonal, every, split_axis=0, concat_axis=0, tiled=True)
-    diagonal, partner = lax.optimization_barrier((jnp.sum(diagonal, axis=0), partner))
-    diagonal = lax.all_gather(diagonal, every, axis=0, tiled=True)
+    diagonal = lax.all_gather(jnp.sum(diagonal, axis=0), every, axis=0, tiled=True)
+    diagonal, partner = lax.optimization_barrier((diagonal, partner))
     inverse = factor_inverse(diagonal)
 
     col_ids = jnp.arange(blocks, dtype=i32) * td + in_tile
@@ -317,14 +317,15 @@
         pl.BlockSpec((TILE, TILE), lambda a, q, t: (a, q)), "strip",
     )
     piece = lax.psum_scatter(strip_part, plane, scatter_dimension=0, tiled=True)
-    pieces = lax.all_gather(piece, "col", axis=0)
+    pieces = jnp.broadcast_to(piece[None], (blocks,) + piece.shape)
+    pieces = lax.all_to_all(pieces, "col", split_axis=0, concat_axis=0, tiled=True)
     strip = lax.all_gather(piece, plane, axis=0, tiled=True)
     pieces = pieces.reshape(chips, piece.shape[0], cores, rd * TILE).transpose(0, 2, 1, 3)
     pieces = pieces.reshape(chips * cores, piece.shape[0], rd * TILE)
     half = lax.all_to_all(pieces, plane, split_axis=0, concat_axis=0, tiled=True)
     half = half.reshape(2 * TILE, rd * TILE)
     wc = lax.dot_general(inverse, strip, (((1,), (0,)), ((), ())), precision=lax.Precision.HIGHEST)
-    wr = lax.dot_general(inverse, half, (((1,), (0,)), ((), ())), precision=lax.Precision.HIGHEST)
+    wr = lax.dot_general(half, inverse, (((0,), (1,)), ((), ())), precision=lax.Precision.HIGHEST)
 
     rr = jnp.broadcast_to(my_rows[:, :, None], (2, rd, cd))
     cc = jnp.broadcast_to(my_cols[:, None, :], (2, rd, cd))
@@ -352,11 +353,12 @@
     return tile_call(
         final_kernel, (rd, cd), (table,), (parent_front, first, second, first, second, wr, wc),
         [pl.BlockSpec((TILE, TILE), lambda i, j, t: (i, j))] + [from_list(n) for n in range(4)] + [
-            pl.BlockSpec((2 * TILE, TILE), lambda i, j, t: (0, i)),
+            pl.BlockSpec((TILE, 2 * TILE), lambda i, j, t: (i, 0)),
             pl.BlockSpec((2 * TILE, TILE), lambda i, j, t: (0, j)),
         ],
         jax.ShapeDtypeStruct(parent_front.shape, F32),
         pl.BlockSpec((TILE, TILE), lambda i, j, t: (i, j)), "final",
+        scratch=[pltpu.VMEM((TILE, 2 * TILE), BF16)] * 2,
     )
 
 

time: 382 us -> 375 us (0.982)
  waiting for transfers between devices: 203 us -> 150 us
  blocking collectives: 0 us -> 38.9 us
    all_to_all x1, waiting for transfers between devices: 45.7 us -> 0.01 us  [body(): lax.all_to_all(outgoing, 'col', split_axis=0, concat_axis=0, tiled=True)]
    all_to_all x0 -> x1, blocking collectives: none -> 38.9 us  [body(): lax.all_to_all(coded, ('child', 'rx'), split_axis=0, concat_axis=0, tiled...]
    reduce_scatter x1, waiting for transfers between devices: 44.4 us -> 13.2 us  [body(): piece = lax.psum_scatter(strip_part, plane, scatter_dimension=0, tiled=True)]
    all_gather x2 -> x1, waiting for transfers between devices: 56.1 us -> 71 us  [body(): lax.all_gather(jnp.sum(diagonal, axis=0), every, axis=0, tiled=True)]
    all_to_all x1, waiting for transfers between devices: 23.4 us -> 34 us  [body(): lax.all_to_all(pieces, 'col', split_axis=0, concat_axis=0, tiled=True)]
  transfers between devices with their start and end apart: 10 -> 9, of which waited for: 7 -> 5; matrix products, arithmetic and copies ran while one was open for 9% -> 10% of each run, Pallas kernels for 15% -> 15%
where the time goes in v5:
time: 375 us; the launch traced here: 372 us
  waiting for transfers between devices  150 us (40%)
  Pallas kernels  106 us (28%)
  blocking collectives  38.9 us (10%)
  starting transfers between devices  18.1 us (5%)
  local copies, waits for them, and re-layouts  16.7 us (4%)
  matrix products  16.3 us (4%)
  between operations  14.5 us (4%)
  other arithmetic  10.7 us (3%)
    all_gather x1, waiting for transfers between devices, body(): lax.all_gather(jnp.sum(diagonal, axis=0), every, axis=0, tiled=True)  71 us
    pallas_call x5, Pallas kernels, tile_call(): pl.pallas_call(kernel, grid_spec=pltpu.PrefetchScalarGridSpec(num_scalar_...  60.2 us
    pallas_call x1, Pallas kernels, factor_inverse(): pl.pallas_call(factor_kernel, out_shape=jax.ShapeDtypeStruct(d.shape, F32...  46 us
    all_to_all x1, blocking collectives, body(): lax.all_to_all(coded, ('child', 'rx'), split_axis=0, concat_axis=0, tiled...  38.9 us
    all_to_all x1, waiting for transfers between devices, body(): lax.all_to_all(pieces, 'col', split_axis=0, concat_axis=0, tiled=True)  34 us
    all_gather x1, waiting for transfers between devices, body(): partner = lax.all_gather(part, ('rx', 'core'), axis=0)  18.8 us
    all_to_all x1, waiting for transfers between devices, body(): lax.all_to_all(diagonal, every, split_axis=0, concat_axis=0, tiled=True)  13.3 us
    reduce_scatter x1, waiting for transfers between devices, body(): piece = lax.psum_scatter(strip_part, plane, scatter_dimension=0, tiled=True)  13.2 us
  transfers between devices with their start and end apart: 9, of which 5 were waited for; matrix products, arithmetic and copies ran while one was open for 10% of the time, Pallas kernels for 15%

profile of v5, /device:TPU:0, one launch (start us, length us, event | category | flops | bytes accessed | tf_op | source)
XLA Modules:
  0.0 371.8 jit_solution(13020529518859001488)
XLA Ops:
  6.5 0.9 select_reduce_fusion.1
  7.7 0.2 fusion
  8.0 0.6 dynamic_slice.59
  9.2 0.6 dynamic_slice.58
  10.4 1.9 dynamic-slice_select_fusion
  12.4 0.7 pad_clamp_fusion.1
  13.0 0.7 broadcast_add_fusion.5
  13.7 0.6 gather_fusion.5
  14.3 0.7 pad_clamp_fusion
  15.0 0.6 gather_fusion.6
  15.8 0.6 gather_fusion.2
  16.4 0.6 gather_fusion.4
  17.0 0.6 gather_fusion.3
  17.7 0.6 gather_fusion.7
  18.4 0.6 stack.90.t
  19.0 18.8 %all-gather.4.cloned.1.call-done.eb.partner = bf16[4,256,1024]{2,1,0:T(8,128)(2,1)} async-done(((bf16[1,256,1024]{2,1,0:T(8,128)(2,1)}), bf16[4,256,1024]{2,1,0:T(8,128)(2,1)}) %all-gather.4.cloned.1.call-update) | async-done | bytes 2097168 | tf_op jit(solution)/shard_map/all_gather | solution.py:247
  37.8 5.6 %diag.1 = f32[512,512]{1,0:T(8,128)} custom-call(s32[8,4]{1,0:T(8,128)} %stack.90.t, f32[1024,1024]{1,0:T(8,128)} %bitcast.128, f32[768,1536]{1,0:T(8,128)} %front.5, bf16[1024,1024]{1,0:T(8,128)(2,1)} %bitcast.130, bf16[4,256,1024]{2,1,0:T(8,128)(2,1)} %all-gather.4.cloned.1.call-done.eb.partner), custom_call_target="tpu_custom_call" | custom-call | tf_op jit(solution)/shard_map/diag/pallas_call | solution.py:30
  43.4 4.5 %all-to-all-start.1 = ((f32[32,16,512]{2,1,0:T(8,128)}), f32[32,16,512]{2,1,0:T(8,128)S(1)}, u32[]{:S(2)}, u32[]{:S(2)}) async-start(f32[32,16,512]{2,1,0:T(8,128)} %bitcast.133), calls=%async_computation.1 | async-start | bytes 2097152 | tf_op jit(solution)/shard_map/all_to_all | solution.py:273
  47.9 0.5 fusion.13
  48.4 11.1 %pick.1 = s16[4,4,272,256]{3,2,1,0:T(8,128)(2,1)} custom-call(s32[4]{0:T(128)} %get-tuple-element.39.idx, f32[1024,1024]{1,0:T(8,128)} %bitcast.129), custom_call_target="tpu_custom_call" | custom-call | tf_op jit(solution)/shard_map/pick/pallas_call | solution.py:30
  59.5 13.3 %all-to-all-done.1 = f32[32,16,512]{2,1,0:T(8,128)S(1)} async-done(((f32[32,16,512]{2,1,0:T(8,128)}), f32[32,16,512]{2,1,0:T(8,128)S(1)}, u32[]{:S(2)}, u32[]{:S(2)}) %all-to-all-start.1) | async-done | bytes 1048608 | tf_op jit(solution)/shard_map/all_to_all | solution.py:273
  72.8 4.6 %all-to-all-start = ((s16[4,4,272,256]{3,2,1,0:T(8,128)(2,1)}), s16[4,4,272,256]{3,2,1,0:T(8,128)(2,1)S(1)}, u32[]{:S(2)}, u32[]{:S(2)}) async-start(s16[4,4,272,256]{3,2,1,0:T(8,128)(2,1)} %pick.1), calls=%async_computation | async-start | bytes 4456448 | tf_op jit(solution)/shard_map/all_to_all | solution.py:241
  77.4 0.6 fusion.25
  78.0 1.2 compare_select_fusion.4
  79.2 0.7 reduce_sum.39
  80.0 0.2 fusion.6
  81.1 0.2 fusion.7
  81.3 0.6 gather_fusion
  82.0 0.6 gather_fusion.1
  82.6 0.6 stack.91.t
  83.3 0.6 multiply_bitcast_fusion.fac
  83.9 71.0 %all-gather.6.cloned.1.call-done.a_in = f32[512,512]{1,0:T(8,128)} async-done(((f32[16,512]{1,0:T(8,128)}), f32[512,512]{1,0:T(8,128)}) %all-gather.6.cloned.1.call-update) | async-done | bytes 1048592 | tf_op jit(solution)/shard_map/all_gather | solution.py:274
  154.9 1.4 copy-done.2
  156.2 15.5 %update.1 = (f32[4,256,1024]{2,1,0:T(8,128)}, s16[4,272,1024]{2,1,0:T(8,128)(2,1)}) custom-call(s32[4]{0:T(128)} %get-tuple-element.41.rows, s32[4,4]{1,0:T(4,128)} %multiply_bitcast_fusion.fac, s16[4,4,272,256]{3,2,1,0:T(8,128)(2,1)} %copy-done.2, bf16[1024,1024]{1,0:T(8,128)(2,1)} %bitcast.131, bf16[4,256,1024]{2,1,0:T(8,128)(2,1)} %all-gather.4.cloned.1.call-done.eb.partner), custom_call_target="tpu_custom_call" | custom-call | tf_op jit(solution)/shard_map/update/pallas_call | solution.py:30
  171.7 9.4 %strip.1 = f32[512,1536]{1,0:T(8,128)} custom-call(s32[5,12]{1,0:T(8,128)} %stack.91.t, f32[4,256,1024]{2,1,0:T(8,128)} %get-tuple-element.11.upd, f32[768,1536]{1,0:T(8,128)} %front.5), custom_call_target="tpu_custom_call" | custom-call | tf_op jit(solution)/shard_map/strip/pallas_call | solution.py:30
  181.1 38.9 %all_to_all.25.a0.a1 = s16[4,272,1024]{2,1,0:T(8,128)(2,1)S(1)} all-to-all(s16[4,272,1024]{2,1,0:T(8,128)(2,1)} %get-tuple-element.10), channel_id=1, replica_groups=mesh['child'=2,'rx'=2,'core'=2,'col'=4] {'child','rx'}, dimensions={0} | all-to-all | bytes 4456448 | tf_op jit(solution)/shard_map/all_to_all | solution.py:296
  220.0 13.2 %reduce-scatter.2.cloned.1.call-done = f32[64,1536]{1,0:T(8,128)} async-done(((f32[512,1536]{1,0:T(8,128)}), f32[64,1536]{1,0:T(8,128)}) %reduce-scatter.2.cloned.1.call-update) | async-done | bytes 393232 | tf_op jit(solution)/shard_map/reduce_scatter | solution.py:319
  233.2 2.3 broadcast_in_dim.184
  235.5 4.6 %all-to-all-start.3 = ((f32[4,64,1536]{2,1,0:T(8,128)}), f32[4,64,1536]{2,1,0:T(8,128)}, u32[]{:S(2)}, u32[]{:S(2)}) async-start(f32[4,64,1536]{2,1,0:T(8,128)} %broadcast_in_dim.184), calls=%async_computation.4 | async-start | bytes 3145728 | tf_op jit(solution)/shard_map/all_to_all | solution.py:321
  241.8 1.2 stack.89.t
  243.0 34.0 %all-to-all-done.3 = f32[4,64,1536]{2,1,0:T(8,128)} async-done(((f32[4,64,1536]{2,1,0:T(8,128)}), f32[4,64,1536]{2,1,0:T(8,128)}, u32[]{:S(2)}, u32[]{:S(2)}) %all-to-all-start.3) | async-done | bytes 1572896 | tf_op jit(solution)/shard_map/all_to_all | solution.py:321
  277.0 1.5 fusion.24
  278.5 1.3 pad_maximum_fusion
  279.8 4.5 %all-to-all-start.4 = ((f32[8,64,768]{2,1,0:T(8,128)}), f32[8,64,768]{2,1,0:T(8,128)}, u32[]{:S(2)}, u32[]{:S(2)}) async-start(f32[8,64,768]{2,1,0:T(8,128)} %bitcast.132), calls=%async_computation.5 | async-start | bytes 3145728 | tf_op jit(solution)/shard_map/all_to_all | solution.py:325
  284.3 46.0 %factor.1 = f32[512,512]{1,0:T(8,128)} custom-call(f32[512,512]{1,0:T(8,128)} %all-gather.6.cloned.1.call-done.a_in), custom_call_target="tpu_custom_call" | custom-call | flops 40000000000 | bytes 2097152 | tf_op jit(solution)/shard_map/factor/pallas_call | solution.py:183
  330.3 8.0 %fusion.26.wr = f32[768,512]{1,0:T(8,128)} fusion(f32[512,768]{1,0:T(8,128)} %bitcast.27, f32[512,512]{1,0:T(8,128)} %factor.1), kind=kOutput, calls=%fused_computation.147 | convolution fusion | flops 2415919104 | bytes 4194304 | tf_op jit(solution)/shard_map/dot_general | solution.py:328
  338.3 8.3 %fusion.27.wc = f32[512,1536]{1,0:T(8,128)} fusion(f32[512,512]{1,0:T(8,128)S(1)} %copy-done.3, f32[512,1536]{1,0:T(8,128)} %all-gather.8.cloned.1.call-done), kind=kOutput, calls=%fused_computation.148 | convolution fusion | flops 4831838208 | bytes 7340032 | tf_op jit(solution)/shard_map/dot_general | solution.py:327
  346.6 18.7 %final.1 = f32[768,1536]{1,0:T(8,128)} custom-call(s32[13,18]{1,0:T(8,128)} %stack.89.t, f32[768,1536]{1,0:T(8,128)} %front.5, s16[4,272,1024]{2,1,0:T(8,128)(2,1)} %copy-done.1, s16[4,272,1024]{2,1,0:T(8,128)(2,1)} %collective-permute-done.b0.b1, s16[4,272,1024]{2,1,0:T(8,128)(2,1)} %copy-done.1, s16[4,272,1024]{2,1,0:T(8,128)(2,1)} %collective-permute-done.b0.b1, ...), custom_call_target="tpu_custom_call" | custom-call | tf_op jit(solution)/shard_map/final/pallas_call | solution.py:30
  (88 shorter events, 3.5 us)
Async XLA Ops:
  6.5 11.1 %copy-start = (s32[2,16,16]{2,1,0:T(8,128)S(1)}, s32[2,16,16]{2,1,0:T(8,128)}, u32[]{:S(2)}) copy-start(s32[2,16,16]{2,1,0:T(8,128)} %param.10) | copy-start | bytes 6148
  6.5 31.3 %all-gather.4.cloned.1.call-start = ((), (), s32[]{:S(2)}) async-start(), calls=%async_computation.6 | async-start | bytes 2621440 | tf_op jit(solution)/shard_map/all_gather | solution.py:247
  43.4 29.4 %all-to-all-start.1 = ((f32[32,16,512]{2,1,0:T(8,128)}), f32[32,16,512]{2,1,0:T(8,128)S(1)}, u32[]{:S(2)}, u32[]{:S(2)}) async-start(f32[32,16,512]{2,1,0:T(8,128)} %bitcast.133), calls=%async_computation.1 | async-start | bytes 2097152 | tf_op jit(solution)/shard_map/all_to_all | solution.py:273
  59.5 17.9 %copy-start.4 = (s32[24]{0:T(128)S(1)}, s32[24]{0:T(128)}, u32[]{:S(2)}) copy-start(s32[24]{0:T(128)} %param.12) | copy-start | bytes 292
  72.8 82.1 %all-to-all-start = ((s16[4,4,272,256]{3,2,1,0:T(8,128)(2,1)}), s16[4,4,272,256]{3,2,1,0:T(8,128)(2,1)S(1)}, u32[]{:S(2)}, u32[]{:S(2)}) async-start(s16[4,4,272,256]{3,2,1,0:T(8,128)(2,1)} %pick.1), calls=%async_computation | async-start | bytes 4456448 | tf_op jit(solution)/shard_map/all_to_all | solution.py:241
  77.3 77.5 %all-gather.6.cloned.1.call-start = ((), (), s32[]{:S(2)}) async-start(), calls=%async_computation.7 | async-start | bytes 1081344 | tf_op jit(solution)/shard_map/all_gather | solution.py:274
  79.9 153.2 %reduce-scatter.2.cloned.1.call-start = ((), (), s32[]{:S(2)}) async-start(), calls=%async_computation.8 | async-start | bytes 3538944 | tf_op jit(solution)/shard_map/reduce_scatter | solution.py:319
  154.9 1.4 copy-start.2
  220.0 23.0 %copy-start.1 = (s16[4,272,1024]{2,1,0:T(8,128)(2,1)}, s16[4,272,1024]{2,1,0:T(8,128)(2,1)S(1)}, u32[]{:S(2)}) copy-start(s16[4,272,1024]{2,1,0:T(8,128)(2,1)S(1)} %all_to_all.25.a0.a1) | copy-start | bytes 6684676
  235.5 41.5 %all-to-all-start.3 = ((f32[4,64,1536]{2,1,0:T(8,128)}), f32[4,64,1536]{2,1,0:T(8,128)}, u32[]{:S(2)}, u32[]{:S(2)}) async-start(f32[4,64,1536]{2,1,0:T(8,128)} %broadcast_in_dim.184), calls=%async_computation.4 | async-start | bytes 3145728 | tf_op jit(solution)/shard_map/all_to_all | solution.py:321
  240.1 98.2 %all-gather.8.cloned.1.call-start = ((), (), s32[]{:S(2)}) async-start(), calls=%async_computation.9 | async-start | bytes 3538944 | tf_op jit(solution)/shard_map/all_gather | solution.py:322
  243.0 103.6 %collective-permute-start = (s16[4,272,1024]{2,1,0:T(8,128)(2,1)S(1)}, s16[4,272,1024]{2,1,0:T(8,128)(2,1)}, u32[]{:S(2)}, u32[]{:S(2)}) collective-permute-start(s16[4,272,1024]{2,1,0:T(8,128)(2,1)S(1)} %all_to_all.25.a0.a1), channel_id=1, source_target_pairs={{0,4},{4,0},{1,5},{5,1},{2,6},{6,2},{3,7},{7,3},{8,12},{12,8},{9,1... | collective-permute-start | bytes 6684680 | tf_op jit(solution)/shard_map/ppermute | solution.py:297
  279.8 50.5 %all-to-all-start.4 = ((f32[8,64,768]{2,1,0:T(8,128)}), f32[8,64,768]{2,1,0:T(8,128)}, u32[]{:S(2)}, u32[]{:S(2)}) async-start(f32[8,64,768]{2,1,0:T(8,128)} %bitcast.132), calls=%async_computation.5 | async-start | bytes 3145728 | tf_op jit(solution)/shard_map/all_to_all | solution.py:325
  330.3 8.0 %copy-start.3 = (f32[512,512]{1,0:T(8,128)S(1)}, f32[512,512]{1,0:T(8,128)}, u32[]{:S(2)}) copy-start(f32[512,512]{1,0:T(8,128)} %factor.1) | copy-start | bytes 3145732
Sparse Core Ops, SparseCore 0:
  12.5 25.2 all-gather.3
  81.1 73.6 all-gather.5
  181.2 51.9 reduce-scatter.1
  242.5 32.6 all-gather.7
